TPU v7x, 32 devices: a whole 2x2x4 slice. The times are simulated.
32 devices in a mesh: seq: 8 (over z, y), tp: 4 (over x, core).
Axes of the slice: x: 2, y: 2, z: 4, core: 2. Of those that a mesh axis runs over, the one named last changes fastest.
Arguments:
- queries: bfloat16 [1024, 4096], P('seq', 'tp'), may hold values from -128 to 128
- keys: bfloat16 [1024, 4096], P('seq', 'tp'), may hold values from -6 to 6
- values: bfloat16 [1024, 4096], P('seq', 'tp'), may hold values from -18 to 18
- residual_in: bfloat16 [1024, 4096], P('seq', 'tp'), may hold values from -6 to 6
- norm_gain: float32 [4096], replicated, may hold values from 0.1 to 1.9
- routing: int32 [8, 1], replicated, may hold values from 0 to 3; in each aligned block of 8 rows (0 to 7, 8 to 15, ...) at most 4 rows name the same one
- gate_weight: bfloat16 [8, 4096, 512], P('seq', None, 'tp'), may hold values from -0.09375 to 0.09375
- up_weight: bfloat16 [8, 4096, 512], P('seq', None, 'tp'), may hold values from -0.09375 to 0.09375
- down_weight: bfloat16 [8, 512, 4096], P('seq', None, 'tp'), may hold values from -0.1875 to 0.1875
Outputs:
- mixed: bfloat16 [1024, 4096], P('seq', 'tp')
Inputs may be any that keep to these rules, and one draw needn't show every extreme that they name: `routing`: every expert is named by some block; no expert by more than 4 blocks, and one by exactly 4.
All inputs are finite; a program needn't handle non-finite values.
Results may differ from a plain program's by a relative error of at most 0.006.
Values may be sent and summed in bfloat16 or wider, within the bound.
A program may use at most 64 MiB of HBM per device.

v0:
```python
import math

import jax
import jax.numpy as jnp
from jax import lax
from jax.sharding import PartitionSpec as P

HEAD_DIM = 128
BLOCK = 128
WINDOW = 512


epsilon = 1e-05
masked_score = -1e30


def shifted(block, axis, distance):
    devices = range(lax.axis_size(axis))
    route = [(i - distance, i) for i in devices if i - distance in devices]
    return lax.ppermute(block, axis, route)


def local(
    queries, keys, values, residual_in, norm_gain, routing, gate_weight, up_weight, down_weight
):
    seq_count = lax.axis_size("seq")
    seq_place = lax.axis_index("seq")
    tok_rows = queries.shape[0]
    feat_width = queries.shape[1]
    head_count = feat_width // HEAD_DIM
    prior_count = (WINDOW - 1) // tok_rows + 1
    earlier_keys = []
    earlier_values = []
    for distance in range(1, prior_count + 1):
        moved_keys, moved_values = shifted((keys, values), "seq", distance)
        earlier_keys.insert(0, moved_keys)
        earlier_values.insert(0, moved_values)
    key_all = jnp.concatenate(earlier_keys + [keys], axis=0).reshape(-1, head_count, HEAD_DIM)
    value_all = jnp.concatenate(earlier_values + [values], axis=0).reshape(-1, head_count, HEAD_DIM)
    query_heads = queries.reshape(tok_rows, head_count, HEAD_DIM)
    query_pos = seq_place * tok_rows + jnp.arange(tok_rows, dtype=jnp.int32)
    key_pos = (
        seq_place * tok_rows
        - prior_count * tok_rows
        + jnp.arange((prior_count + 1) * tok_rows, dtype=jnp.int32)
    )
    visible = (
        (key_pos[None, :] >= 0)
        & (key_pos[None, :] <= query_pos[:, None])
        & (key_pos[None, :] > query_pos[:, None] - WINDOW)
    )
    scores = jnp.einsum(
        "qhd,khd->hqk", query_heads, key_all, preferred_element_type=jnp.float32
    ) * (1.0 / math.sqrt(HEAD_DIM))
    scores = jnp.where(visible[None], scores, masked_score)
    top_score = jnp.max(scores, axis=2, keepdims=True)
    expo = jnp.exp(scores - top_score)
    weights_soft = (expo / jnp.sum(expo, axis=2, keepdims=True)).astype(jnp.bfloat16)
    attended = jnp.einsum(
        "hqk,khd->qhd", weights_soft, value_all, preferred_element_type=jnp.float32
    ).reshape(tok_rows, feat_width)
    stream = (residual_in.astype(jnp.float32) + attended).astype(jnp.bfloat16)
    send_width = stream.shape[1]
    blocks_dev = tok_rows // BLOCK
    piece_rows = BLOCK // seq_count
    spread_in = stream.reshape(blocks_dev, seq_count, piece_rows, send_width)
    spread_out = lax.all_to_all(spread_in, "seq", split_axis=1, concat_axis=0, tiled=True)
    block_count = blocks_dev * seq_count
    spread_rows = spread_out.reshape(block_count, piece_rows, send_width)
    expert_ids = routing[:, 0]
    expert_count = seq_count // 2
    most_blocks = min(2 * block_count // expert_count, block_count - expert_count + 1)
    order_index = jnp.arange(block_count, dtype=jnp.int32)
    same_expert = expert_ids[None, :] == expert_ids[:, None]
    rank_of = jnp.sum(same_expert & (order_index[None, :] < order_index[:, None]), axis=1)
    expert_range = jnp.arange(expert_count, dtype=jnp.int32)
    slot_range = jnp.arange(most_blocks, dtype=jnp.int32)
    selector = (
        (expert_ids[None, None, :] == expert_range[:, None, None])
        & (rank_of[None, None, :] == slot_range[None, :, None])
    ).astype(jnp.bfloat16)
    picked = jnp.einsum(
        "erb,bqf->erqf", selector, spread_rows, preferred_element_type=jnp.float32
    ).astype(jnp.bfloat16)
    outgoing = jnp.broadcast_to(
        picked[:, None], (expert_count, 2, most_blocks, piece_rows, send_width)
    )
    outgoing = outgoing.reshape(seq_count, most_blocks, piece_rows, send_width)
    features_full = lax.all_gather(
        lax.all_to_all(outgoing, "seq", split_axis=0, concat_axis=0, tiled=True),
        "tp",
        axis=3,
        tiled=True,
    )
    source_count = features_full.shape[0]
    slot_count = features_full.shape[1]
    stream_f32 = features_full.astype(jnp.float32)
    mean_square = jnp.mean(stream_f32 * stream_f32, axis=3, keepdims=True)
    normed = (stream_f32 * lax.rsqrt(mean_square + epsilon) * norm_gain).astype(jnp.bfloat16)
    normed = normed.reshape(-1, normed.shape[3])
    gate_val = jnp.dot(normed, gate_weight[0], preferred_element_type=jnp.float32)
    up_val = jnp.dot(normed, up_weight[0], preferred_element_type=jnp.float32)
    hidden = (jax.nn.silu(gate_val) * up_val).astype(jnp.bfloat16)
    hidden_half = lax.all_gather(hidden, "tp", axis=1, tiled=True)
    partial_value = jnp.dot(hidden_half, down_weight[0], preferred_element_type=jnp.float32).astype(
        jnp.bfloat16
    )
    partial_value = partial_value.reshape(source_count, slot_count, piece_rows, feat_width)
    returned = lax.all_to_all(partial_value, "seq", split_axis=0, concat_axis=0, tiled=True)
    returned = returned.reshape(expert_count, 2, most_blocks, piece_rows * feat_width)
    combined = jnp.einsum("erb,epry->pby", selector, returned, preferred_element_type=jnp.float32)
    residual_rows = spread_rows
    residual_rows = residual_rows.reshape(block_count, piece_rows * feat_width).astype(jnp.float32)
    finished = (residual_rows + combined[0] + combined[1]).astype(jnp.bfloat16)
    finished = finished.reshape(seq_count, blocks_dev, piece_rows, feat_width)
    restored = lax.all_to_all(finished, "seq", split_axis=0, concat_axis=2, tiled=True)
    return restored.reshape(tok_rows, feat_width)


def solution(mesh):
    in_specs = (
        P("seq", "tp"),
        P("seq", "tp"),
        P("seq", "tp"),
        P("seq", "tp"),
        P(),
        P(),
        P("seq", None, "tp"),
        P("seq", None, "tp"),
        P("seq", None, "tp"),
    )
    out_specs = P("seq", "tp")
    return jax.shard_map(local, mesh=mesh, in_specs=in_specs, out_specs=out_specs, check_vma=False)
```

profile of v0, /device:TPU:0, one launch (start us, length us, event | category | flops | bytes accessed | tf_op | source)
XLA Modules:
  0.0 241.6 jit_solution(3247375718522267183)
XLA Ops:
  6.5 1.2 copy.46
  7.8 4.9 %collective-permute-start.7 = (bf16[128,1024]{0,1:T(8,128)(2,1)S(1)}, bf16[128,1024]{0,1:T(8,128)(2,1)S(1)}, u32[]{:S(2)}, u32[]{:S(2)}) collective-permute-start(bf16[128,1024]{0,1:T(8,128)(2,1)S(1)} %copy.46), channel_id=1, source_target_pairs={{0,4},{4,8},{8,12},{12,16},{16,20},{20,24},{24,28},{1,5},{5,9},{9,... | collective-permute-start | bytes 786440 | tf_op jit(solution)/shard_map/ppermute | solution.py:20
  12.7 3.5 %collective-permute-start.6 = (bf16[128,1024]{0,1:T(8,128)(2,1)S(1)}, bf16[128,1024]{0,1:T(8,128)(2,1)S(1)}, u32[]{:S(2)}, u32[]{:S(2)}) collective-permute-start(bf16[128,1024]{0,1:T(8,128)(2,1)S(1)} %copy.46), channel_id=1, source_target_pairs={{0,8},{4,12},{8,16},{12,20},{16,24},{20,28},{1,9},{5,13},{9,17},{1... | collective-permute-start | bytes 786440 | tf_op jit(solution)/shard_map/ppermute | solution.py:20
  16.2 4.2 %collective-permute-start.2 = (bf16[128,1024]{1,0:T(8,128)(2,1)}, bf16[128,1024]{1,0:T(8,128)(2,1)}, u32[]{:S(2)}, u32[]{:S(2)}) collective-permute-start(bf16[128,1024]{1,0:T(8,128)(2,1)} %param.11), channel_id=1, source_target_pairs={{0,8},{4,12},{8,16},{12,20},{16,24},{20,28},{1,9},{5,13},{9,17},{1... | collective-permute-start | bytes 786440 | tf_op jit(solution)/shard_map/ppermute | solution.py:20
  20.4 2.9 %collective-permute-start.1 = (bf16[128,1024]{1,0:T(8,128)(2,1)}, bf16[128,1024]{1,0:T(8,128)(2,1)}, u32[]{:S(2)}, u32[]{:S(2)}) collective-permute-start(bf16[128,1024]{1,0:T(8,128)(2,1)} %param.11), channel_id=1, source_target_pairs={{0,12},{4,16},{8,20},{12,24},{16,28},{1,13},{5,17},{9,21},{13,25},... | collective-permute-start | bytes 786440 | tf_op jit(solution)/shard_map/ppermute | solution.py:20
  23.3 1.3 collective-permute-start
  24.6 0.2 compare_and_fusion
  24.9 13.6 %collective-permute-done = bf16[128,1024]{1,0:T(8,128)(2,1)S(1)} collective-permute-done((bf16[128,1024]{1,0:T(8,128)(2,1)}, bf16[128,1024]{1,0:T(8,128)(2,1)S(1)}, u32[]{:S(2)}, u32[]{:S(2)}) %collective-permute-start) | collective-permute-done | bytes 262176 | tf_op jit(solution)/shard_map/ppermute | solution.py:20
  38.4 0.7 copy-done.5
  39.1 5.8 %collective-permute-start.3 = (bf16[128,1024]{1,0:T(8,128)(2,1)}, bf16[128,1024]{1,0:T(8,128)(2,1)S(1)}, u32[]{:S(2)}, u32[]{:S(2)}) collective-permute-start(bf16[128,1024]{1,0:T(8,128)(2,1)} %param.11), channel_id=1, source_target_pairs={{0,4},{4,8},{8,12},{12,16},{16,20},{20,24},{24,28},{1,5},{5,9},{9,... | collective-permute-start | bytes 786440 | tf_op jit(solution)/shard_map/ppermute | solution.py:20
  45.0 1.0 constant_dynamic-update-slice_fusion.4
  46.0 0.0 collective-permute-done.1
  46.0 16.3 %collective-permute-start.5 = (bf16[128,1024]{0,1:T(8,128)(2,1)S(1)}, bf16[128,1024]{0,1:T(8,128)(2,1)}, u32[]{:S(2)}, u32[]{:S(2)}) collective-permute-start(bf16[128,1024]{0,1:T(8,128)(2,1)S(1)} %copy.46), channel_id=1, source_target_pairs={{0,12},{4,16},{8,20},{12,24},{16,28},{1,13},{5,17},{9,21},{13,25},... | collective-permute-start | bytes 786440 | tf_op jit(solution)/shard_map/ppermute | solution.py:20
  62.3 1.0 constant_dynamic-update-slice_fusion.3
  63.2 0.0 collective-permute-done.2
  63.2 4.0 %collective-permute-start.4 = (bf16[128,1024]{0,1:T(8,128)(2,1)S(1)}, bf16[128,1024]{0,1:T(8,128)(2,1)S(1)}, u32[]{:S(2)}, u32[]{:S(2)}) collective-permute-start(bf16[128,1024]{0,1:T(8,128)(2,1)S(1)} %copy.46), channel_id=1, source_target_pairs={{0,16},{4,20},{8,24},{12,28},{1,17},{5,21},{9,25},{13,29},{2,18},{... | collective-permute-start | bytes 786440 | tf_op jit(solution)/shard_map/ppermute | solution.py:20
  67.3 1.0 constant_dynamic-update-slice_fusion.2
  68.2 0.0 collective-permute-done.3
  68.3 0.0 copy-done.4
  68.3 2.8 %collective-permute-done.4 = bf16[128,1024]{0,1:T(8,128)(2,1)S(1)} collective-permute-done((bf16[128,1024]{0,1:T(8,128)(2,1)S(1)}, bf16[128,1024]{0,1:T(8,128)(2,1)S(1)}, u32[]{:S(2)}, u32[]{:S(2)}) %collective-permute-start.4) | collective-permute-done | bytes 262176 | tf_op jit(solution)/shard_map/ppermute | solution.py:20
  71.2 0.7 constant_dynamic-update-slice_fusion.9
  71.9 1.4 copy.45
  73.3 0.0 collective-permute-done.5
  73.3 1.7 constant_dynamic-update-slice_fusion.8
  75.1 0.0 collective-permute-done.6
  75.1 0.8 constant_dynamic-update-slice_fusion.7
  75.8 0.0 collective-permute-done.7
  75.8 0.7 constant_dynamic-update-slice_fusion.6
  76.6 0.8 constant_dynamic-update-slice_fusion.5
  77.4 0.0 copy-done.10
  77.4 4.0 %fusion.40 = (f32[8,128]{1,0:T(8,128)S(1)}, f32[8,128,640]{1,2,0:T(8,128)}) fusion(pred[128,640]{0,1:T(8,128)(4,1)S(1)} %compare_and_fusion, bf16[640,8,128]{0,2,1:T(8,128)(2,1)} %bitcast.84, bf16[128,1024]{1,0:T(8,128)(2,1)S(1)} %copy-done.10), kind=kOutput, calls=%fused_computation.65 | convolution fusion | flops 170394240 | bytes 4280320 | tf_op jit(solution)/shard_map/sub | solution.py:57
  81.4 2.3 fusion.7
  83.7 0.0 copy-start.8
  83.7 0.2 copy.54
  83.9 0.0 copy-done.6
  83.9 0.8 add_convert_fusion
  84.7 15.9 %all-to-all-start = ((bf16[1,8,16,1024]{3,2,0,1:T(8,128)(2,1)}), bf16[1,8,16,1024]{3,2,0,1:T(8,128)(2,1)S(1)}, u32[]{:S(2)}, u32[]{:S(2)}) async-start(bf16[1,8,16,1024]{3,2,0,1:T(8,128)(2,1)} %bitcast.6), calls=%async_computation | async-start | bytes 524288 | tf_op jit(solution)/shard_map/all_to_all | solution.py:67
  100.5 0.0 all-gather.2.cloned.1.call-start
  100.6 0.2 convert_reduce_fusion
  100.8 8.5 %all-to-all-done = bf16[1,8,16,1024]{3,2,0,1:T(8,128)(2,1)S(1)} async-done(((bf16[1,8,16,1024]{3,2,0,1:T(8,128)(2,1)}), bf16[1,8,16,1024]{3,2,0,1:T(8,128)(2,1)S(1)}, u32[]{:S(2)}, u32[]{:S(2)}) %all-to-all-start) | async-done | bytes 262176 | tf_op jit(solution)/shard_map/all_to_all | solution.py:67
  109.3 0.3 convolution_convert_fusion.1
  109.6 0.2 copy.57
  109.8 0.1 broadcast_in_dim.16
  109.9 29.0 %all_to_all.28 = bf16[8,4,16,1024]{3,2,1,0:T(8,128)(2,1)} all-to-all(bf16[8,4,16,1024]{3,2,1,0:T(8,128)(2,1)S(1)} %bitcast.77), channel_id=1, replica_groups=mesh['seq'=8,'tp'=4] {'seq'}, dimensions={0} | all-to-all | bytes 2097152 | tf_op jit(solution)/shard_map/all_to_all | solution.py:90
  138.8 0.0 all-gather.2.cloned.1.call-update
  138.9 0.0 copy-start.7
  138.9 33.6 %all-gather.2.cloned.1.call-done = bf16[8,4,16,4096]{3,2,1,0:T(8,128)(2,1)} async-done(((bf16[8,4,16,1024]{3,2,1,0:T(8,128)(2,1)}), bf16[8,4,16,4096]{3,2,1,0:T(8,128)(2,1)}) %all-gather.2.cloned.1.call-update) | async-done | bytes 4194320 | tf_op jit(solution)/shard_map/all_gather | solution.py:89
  172.4 3.2 %fusion.1 = f32[8,4,16]{2,1,0:T(4,128)S(1)} fusion(bf16[8,4,16,4096]{3,2,1,0:T(8,128)(2,1)} %all-gather.2.cloned.1.call-done), kind=kLoop, calls=%fused_computation.4 | loop fusion | flops 6290944 | bytes 4196352 | tf_op jit(solution)/shard_map/reduce_sum | solution.py:98
  175.7 0.0 copy-done.7
  175.7 0.2 copy-done.1
  175.9 1.7 fusion.3
  177.6 0.0 copy-start.9
  177.6 1.2 fusion.12
  178.8 1.2 fusion.9
  180.1 7.2 %all_gather.7 = bf16[512,512]{1,0:T(8,128)(2,1)S(1)} all-gather(bf16[512,128]{1,0:T(8,128)(2,1)S(1)} %fusion.9), channel_id=1, replica_groups=mesh['seq'=8,'tp'=4] {'tp'}, dimensions={1}, use_global_device_ids=true | all-gather | bytes 655360 | tf_op jit(solution)/shard_map/all_gather | solution.py:104
  187.3 0.0 copy-done
  187.3 0.7 convolution_convert_fusion
  188.0 31.5 %all_to_all.29 = bf16[8,4,16,1024]{3,2,1,0:T(8,128)(2,1)S(1)} all-to-all(bf16[8,4,16,1024]{3,2,1,0:T(8,128)(2,1)S(1)} %bitcast.81), channel_id=1, replica_groups=mesh['seq'=8,'tp'=4] {'seq'}, dimensions={0} | all-to-all | bytes 2097152 | tf_op jit(solution)/shard_map/all_to_all | solution.py:109
  219.6 0.8 reshape.236
  220.4 0.6 convolution_bitcast_fusion
  221.0 0.1 fusion.39
  221.1 0.6 fusion.16
  221.7 12.4 %all_to_all.30 = bf16[8,1,16,1024]{3,2,1,0:T(8,128)(2,1)S(1)} all-to-all(bf16[8,1,16,1024]{3,2,1,0:T(8,128)(2,1)S(1)} %fusion.16), channel_id=1, replica_groups=mesh['seq'=8,'tp'=4] {'seq'}, dimensions={0} | all-to-all | bytes 524288 | tf_op jit(solution)/shard_map/all_to_all | solution.py:116
  234.1 0.7 copy.96
  (19 shorter events, 0.1 us)
Async XLA Ops:
  6.5 180.8 %copy-start = (bf16[1,512,1024]{2,1,0:T(8,128)(2,1)S(1)}, bf16[1,512,1024]{2,1,0:T(8,128)(2,1)}, u32[]{:S(2)}) copy-start(bf16[1,512,1024]{2,1,0:T(8,128)(2,1)} %param.17) | copy-start | bytes 3145732
  6.5 61.8 %copy-start.4 = (bf16[128,1024]{1,0:T(8,128)(2,1)S(1)}, bf16[128,1024]{1,0:T(8,128)(2,1)}, u32[]{:S(2)}) copy-start(bf16[128,1024]{1,0:T(8,128)(2,1)} %param.11) | copy-start | bytes 786436
  7.8 68.1 %collective-permute-start.7 = (bf16[128,1024]{0,1:T(8,128)(2,1)S(1)}, bf16[128,1024]{0,1:T(8,128)(2,1)S(1)}, u32[]{:S(2)}, u32[]{:S(2)}) collective-permute-start(bf16[128,1024]{0,1:T(8,128)(2,1)S(1)} %copy.46), channel_id=1, source_target_pairs={{0,4},{4,8},{8,12},{12,16},{16,20},{20,24},{24,28},{1,5},{5,9},{9,... | collective-permute-start | bytes 786440 | tf_op jit(solution)/shard_map/ppermute | solution.py:20
  12.7 62.4 %collective-permute-start.6 = (bf16[128,1024]{0,1:T(8,128)(2,1)S(1)}, bf16[128,1024]{0,1:T(8,128)(2,1)S(1)}, u32[]{:S(2)}, u32[]{:S(2)}) collective-permute-start(bf16[128,1024]{0,1:T(8,128)(2,1)S(1)} %copy.46), channel_id=1, source_target_pairs={{0,8},{4,12},{8,16},{12,20},{16,24},{20,28},{1,9},{5,13},{9,17},{1... | collective-permute-start | bytes 786440 | tf_op jit(solution)/shard_map/ppermute | solution.py:20
  16.2 47.1 %collective-permute-start.2 = (bf16[128,1024]{1,0:T(8,128)(2,1)}, bf16[128,1024]{1,0:T(8,128)(2,1)}, u32[]{:S(2)}, u32[]{:S(2)}) collective-permute-start(bf16[128,1024]{1,0:T(8,128)(2,1)} %param.11), channel_id=1, source_target_pairs={{0,8},{4,12},{8,16},{12,20},{16,24},{20,28},{1,9},{5,13},{9,17},{1... | collective-permute-start | bytes 786440 | tf_op jit(solution)/shard_map/ppermute | solution.py:20
  20.4 25.6 %collective-permute-start.1 = (bf16[128,1024]{1,0:T(8,128)(2,1)}, bf16[128,1024]{1,0:T(8,128)(2,1)}, u32[]{:S(2)}, u32[]{:S(2)}) collective-permute-start(bf16[128,1024]{1,0:T(8,128)(2,1)} %param.11), channel_id=1, source_target_pairs={{0,12},{4,16},{8,20},{12,24},{16,28},{1,13},{5,17},{9,21},{13,25},... | collective-permute-start | bytes 786440 | tf_op jit(solution)/shard_map/ppermute | solution.py:20
  23.3 15.2 %collective-permute-start = (bf16[128,1024]{1,0:T(8,128)(2,1)}, bf16[128,1024]{1,0:T(8,128)(2,1)S(1)}, u32[]{:S(2)}, u32[]{:S(2)}) collective-permute-start(bf16[128,1024]{1,0:T(8,128)(2,1)} %param.11), channel_id=1, source_target_pairs={{0,16},{4,20},{8,24},{12,28},{1,17},{5,21},{9,25},{13,29},{2,18},{... | collective-permute-start | bytes 786440 | tf_op jit(solution)/shard_map/ppermute | solution.py:20
  38.4 0.7 copy-start.5
  39.1 29.1 %collective-permute-start.3 = (bf16[128,1024]{1,0:T(8,128)(2,1)}, bf16[128,1024]{1,0:T(8,128)(2,1)S(1)}, u32[]{:S(2)}, u32[]{:S(2)}) collective-permute-start(bf16[128,1024]{1,0:T(8,128)(2,1)} %param.11), channel_id=1, source_target_pairs={{0,4},{4,8},{8,12},{12,16},{16,20},{20,24},{24,28},{1,5},{5,9},{9,... | collective-permute-start | bytes 786440 | tf_op jit(solution)/shard_map/ppermute | solution.py:20
  46.0 27.4 %collective-permute-start.5 = (bf16[128,1024]{0,1:T(8,128)(2,1)S(1)}, bf16[128,1024]{0,1:T(8,128)(2,1)}, u32[]{:S(2)}, u32[]{:S(2)}) collective-permute-start(bf16[128,1024]{0,1:T(8,128)(2,1)S(1)} %copy.46), channel_id=1, source_target_pairs={{0,12},{4,16},{8,20},{12,24},{16,28},{1,13},{5,17},{9,21},{13,25},... | collective-permute-start | bytes 786440 | tf_op jit(solution)/shard_map/ppermute | solution.py:20
  63.2 7.9 %collective-permute-start.4 = (bf16[128,1024]{0,1:T(8,128)(2,1)S(1)}, bf16[128,1024]{0,1:T(8,128)(2,1)S(1)}, u32[]{:S(2)}, u32[]{:S(2)}) collective-permute-start(bf16[128,1024]{0,1:T(8,128)(2,1)S(1)} %copy.46), channel_id=1, source_target_pairs={{0,16},{4,20},{8,24},{12,28},{1,17},{5,21},{9,25},{13,29},{2,18},{... | collective-permute-start | bytes 786440 | tf_op jit(solution)/shard_map/ppermute | solution.py:20
  73.3 4.0 %copy-start.10 = (bf16[128,1024]{1,0:T(8,128)(2,1)S(1)}, bf16[128,1024]{1,0:T(8,128)(2,1)}, u32[]{:S(2)}) copy-start(bf16[128,1024]{1,0:T(8,128)(2,1)} %param.9) | copy-start | bytes 786436
  77.4 4.0 %copy-start.2 = (bf16[640,1024]{0,1:T(8,128)(2,1)S(1)}, bf16[640,1024]{0,1:T(8,128)(2,1)}, u32[]{:S(2)}) copy-start(bf16[640,1024]{0,1:T(8,128)(2,1)} %copy.45) | copy-start | bytes 3932164
  81.4 2.5 %copy-start.6 = (bf16[128,1024]{1,0:T(8,128)(2,1)S(1)}, bf16[128,1024]{1,0:T(8,128)(2,1)}, u32[]{:S(2)}) copy-start(bf16[128,1024]{1,0:T(8,128)(2,1)} %param.12) | copy-start | bytes 786436
  83.7 16.9 %copy-start.8 = (s32[8,1]{0,1:T(1,128)S(1)}, s32[8,1]{0,1:T(1,128)}, u32[]{:S(2)}) copy-start(s32[8,1]{0,1:T(1,128)} %param.14) | copy-start | bytes 100
  84.7 24.6 %all-to-all-start = ((bf16[1,8,16,1024]{3,2,0,1:T(8,128)(2,1)}), bf16[1,8,16,1024]{3,2,0,1:T(8,128)(2,1)S(1)}, u32[]{:S(2)}, u32[]{:S(2)}) async-start(bf16[1,8,16,1024]{3,2,0,1:T(8,128)(2,1)} %bitcast.6), calls=%async_computation | async-start | bytes 524288 | tf_op jit(solution)/shard_map/all_to_all | solution.py:67
  100.5 71.9 %all-gather.2.cloned.1.call-start = ((), (), s32[]{:S(2)}) async-start(), calls=%async_computation.4 | async-start | bytes 5242880 | tf_op jit(solution)/shard_map/all_gather | solution.py:89
  138.9 36.8 %copy-start.7 = (f32[4096]{0:T(1024)S(1)}, f32[4096]{0:T(1024)}, u32[]{:S(2)}) copy-start(f32[4096]{0:T(1024)} %param.13) | copy-start | bytes 49156
  172.4 3.4 %copy-start.1 = (bf16[8,4,16,4096]{3,2,1,0:T(8,128)(2,1)S(1)}, bf16[8,4,16,4096]{3,2,1,0:T(8,128)(2,1)}, u32[]{:S(2)}) copy-start(bf16[8,4,16,4096]{3,2,1,0:T(8,128)(2,1)} %all-gather.2.cloned.1.call-done) | copy-start | bytes 12582916
  175.9 1.7 copy-start.3
  177.6 1.3 copy-start.9
Sparse Core Ops, SparseCore 0:
  139.0 33.4 all-gather.1
where the time goes:
time: 242 us
  blocking collectives  80.1 us (33%)
  starting transfers between devices  58.8 us (24%)
  waiting for transfers between devices  58.5 us (24%)
  between operations  13.7 us (6%)
  local copies, waits for them, and re-layouts  13.3 us (5%)
  matrix products  10.4 us (4%)
  other arithmetic  6.7 us (3%)
    ppermute x8, starting transfers between devices, shifted(): return lax.ppermute(block, axis, route)  42.9 us
    all_gather x1, waiting for transfers between devices, local(): lax.all_gather(lax.all_to_all(outgoing, 'seq', split_axis=0, concat_axis=...  33.6 us
    all_to_all x1, blocking collectives, local(): lax.all_to_all(partial_value, 'seq', split_axis=0, concat_axis=0, tiled=T...  31.5 us
    all_to_all x1, blocking collectives, local(): lax.all_to_all(outgoing, 'seq', split_axis=0, concat_axis=0, tiled=True)  29 us
    ppermute x8, waiting for transfers between devices, shifted(): return lax.ppermute(block, axis, route)  16.4 us
    all_to_all x1, starting transfers between devices, local(): lax.all_to_all(spread_in, 'seq', split_axis=1, concat_axis=0, tiled=True)  15.9 us
    all_to_all x1, blocking collectives, local(): lax.all_to_all(finished, 'seq', split_axis=0, concat_axis=2, tiled=True)  12.4 us
    unnamed x32, local copies, waits for them, and re-layouts  9.76 us
  transfers between devices with their start and end apart: 10, of which 4 were waited for; matrix products, arithmetic and copies ran while one was open for 3% of the time, Pallas kernels for 0%

commit v1 on v0

--- a/solution.py
+++ b/solution.py
@@ -3,6 +3,8 @@
 import jax
 import jax.numpy as jnp
 from jax import lax
+from jax.experimental import pallas as pl
+from jax.experimental.pallas import tpu as pltpu
 from jax.sharding import PartitionSpec as P
 
 HEAD_DIM = 128
@@ -20,7 +22,7 @@
     return lax.ppermute(block, axis, route)
 
 
-def local(
+def local_general(
     queries, keys, values, residual_in, norm_gain, routing, gate_weight, up_weight, down_weight
 ):
     seq_count = lax.axis_size("seq")
@@ -117,6 +119,498 @@
     return restored.reshape(tok_rows, feat_width)
 
 
+BF16 = jnp.bfloat16
+F32 = jnp.float32
+
+
+def remote(src, dst, send_sem, recv_sem, device):
+    return pltpu.make_async_remote_copy(
+        src_ref=src,
+        dst_ref=dst,
+        send_sem=send_sem,
+        recv_sem=recv_sem,
+        device_id=device,
+        device_id_type=pl.DeviceIdType.MESH,
+    )
+
+
+def layer_kernel(
+    planes,
+    most,
+    routing_ref,
+    q_ref,
+    k_ref,
+    v_ref,
+    r_ref,
+    gain_ref,
+    gate_ref,
+    up_ref,
+    down_ref,
+    out_ref,
+    q_buf,
+    r_buf,
+    kv_buf,
+    line_buf,
+    x_buf,
+    w_buf,
+    acc_buf,
+    square_buf,
+    hid_buf,
+    down_buf,
+    mix_buf,
+    up_out,
+    up_in,
+    dn_out,
+    dn_in,
+    fin_buf,
+    pair_s,
+    pair_r,
+    local_s,
+    kvline_s,
+    kvline_r,
+    line_s,
+    line_r,
+    feat_s,
+    feat_r,
+    hid_s,
+    hid_r,
+    ret_s,
+    ret_r,
+    last_s,
+    last_r,
+):
+    rows = q_ref.shape[0]
+    half = q_ref.shape[1] // 2
+    heads = half // HEAD_DIM
+    blocks = 2 * planes
+    me = lax.axis_index("seq")
+    t = lax.axis_index("tp")
+    z = me // 2
+    y = me % 2
+    yo = 1 - y
+    mate = 2 * z + yo
+    tc = t + 1 - 2 * (t % 2)
+    tx = t + 2 - 4 * (t // 2)
+    txc = tx + 1 - 2 * (tx % 2)
+    dev_y, dev_c, dev_x = (mate, t), (me, tc), (me, tx)
+    dev_up, dev_dn = (me + 2, t), (me - 2, t)
+    has_up, has_dn = z < planes - 1, z > 0
+    unsent = []
+
+    barrier = pltpu.get_barrier_semaphore()
+
+    def greet(device):
+        pl.semaphore_signal(
+            barrier, inc=1, device_id=device, device_id_type=pl.DeviceIdType.MESH
+        )
+
+    for device in (dev_y, dev_c, dev_x):
+        greet(device)
+    pl.when(has_up)(lambda: greet(dev_up))
+    pl.when(has_dn)(lambda: greet(dev_dn))
+
+    def cols(which, h):
+        return pl.ds(pl.multiple_of(which * half + h * HEAD_DIM, HEAD_DIM), HEAD_DIM)
+
+    def wide(which):
+        return pl.ds(pl.multiple_of(which * half, half), half)
+
+    stay = []
+    for h in range(heads):
+        stay.append((k_ref.at[:, cols(y, h)], kv_buf.at[0, h, 0, y]))
+        stay.append((v_ref.at[:, cols(y, h)], kv_buf.at[0, h, 1, y]))
+    stay.append((q_ref.at[:, wide(y)], q_buf.at[y]))
+    stay.append((r_ref.at[:, wide(y)], r_buf.at[y]))
+    stay.append((gate_ref.at[0], w_buf.at[:, pl.ds(0, gate_ref.shape[2])]))
+    stay.append((up_ref.at[0], w_buf.at[:, pl.ds(gate_ref.shape[2], gate_ref.shape[2])]))
+    stay.append((down_ref.at[0, :, wide(y)], down_buf.at[y]))
+    stay = [pltpu.make_async_copy(a, b, local_s.at[i]) for i, (a, b) in enumerate(stay)]
+    for copy in stay:
+        copy.start()
+
+    expert = [routing_ref[b, 0] for b in range(blocks)]
+    slot = []
+    for b in range(blocks):
+        count = jnp.int32(0)
+        for j in range(b):
+            count = count + jnp.where(expert[j] == expert[b], 1, 0)
+        slot.append(jnp.minimum(count, most - 1))
+    chosen = []
+    for r in range(most):
+        index = jnp.int32(0)
+        for b in range(blocks):
+            index = jnp.where((expert[b] == z) & (slot[b] == r), b, index)
+        chosen.append(index)
+
+    for dist in (1, 2):
+
+        @pl.when(z < dist)
+        def _():
+            kv_buf[dist] = jnp.zeros(kv_buf.shape[1:], kv_buf.dtype)
+
+    pl.semaphore_wait(
+        barrier, 3 + jnp.where(has_up, 1, 0) + jnp.where(has_dn, 1, 0)
+    )
+
+    def pair_copy(i, src, dst):
+        return remote(src, dst, pair_s.at[i], pair_r.at[i], dev_y)
+
+    swap, landed = [], []
+    for h in range(heads):
+        for n, ref in enumerate((k_ref, v_ref)):
+            i = len(swap)
+            swap.append(pair_copy(i, ref.at[:, cols(yo, h)], kv_buf.at[0, h, n, y]))
+            landed.append(pair_copy(i, kv_buf.at[0, h, n, yo], kv_buf.at[0, h, n, yo]))
+    for ref, buf in ((q_ref, q_buf), (r_ref, r_buf)):
+        i = len(swap)
+        swap.append(pair_copy(i, ref.at[:, wide(yo)], buf.at[y]))
+        landed.append(pair_copy(i, buf.at[yo], buf.at[yo]))
+    i = len(swap)
+    swap.append(pair_copy(i, down_ref.at[0, :, wide(yo)], down_buf.at[y + 2]))
+    landed.append(pair_copy(i, down_buf.at[yo + 2], down_buf.at[yo + 2]))
+    for copy in swap:
+        copy.start()
+        unsent.append((None, copy))
+
+    def kv_copy(dist, h):
+        return remote(
+            kv_buf.at[dist, h],
+            kv_buf.at[dist + 1, h],
+            kvline_s.at[dist, h],
+            kvline_r.at[dist, h],
+            dev_up,
+        )
+
+    def kv_own(h):
+        for i in (2 * h, 2 * h + 1):
+            stay[i].wait()
+            landed[i].wait_recv()
+        pl.when(has_up)(lambda: kv_copy(0, h).start())
+        unsent.append((has_up, kv_copy(0, h)))
+
+    def kv_relay(h):
+        pl.when(has_dn)(lambda: kv_copy(0, h).wait_recv())
+        pl.when(has_dn & has_up)(lambda: kv_copy(1, h).start())
+        unsent.append((has_dn & has_up, kv_copy(1, h)))
+
+    def line_copy(way, plane, h):
+        return remote(
+            line_buf.at[plane, h],
+            line_buf.at[plane, h],
+            line_s.at[way, plane, h],
+            line_r.at[way, plane, h],
+            dev_up if way == 0 else dev_dn,
+        )
+
+    query_at = lax.broadcasted_iota(jnp.int32, (2 * rows, 2 * rows), 0)
+    key_at = lax.broadcasted_iota(jnp.int32, (2 * rows, 2 * rows), 1)
+
+    def attend(h):
+        pl.when(z > 1)(lambda: kv_copy(1, h).wait_recv())
+        at = pl.ds(h * HEAD_DIM, HEAD_DIM)
+        query = q_buf[:, :, at].reshape(2 * rows, HEAD_DIM)
+        parts = []
+        for dist in range(3):
+            key = kv_buf[dist, h, 0].reshape(2 * rows, HEAD_DIM)
+            score = lax.dot_general(
+                query, key, (((1,), (1,)), ((), ())), preferred_element_type=F32
+            ) * (1.0 / math.sqrt(HEAD_DIM))
+            gap = query_at - key_at + 2 * rows * dist
+            seen = (gap >= 0) & (gap < WINDOW) & (jnp.full(gap.shape, z, jnp.int32) >= dist)
+            parts.append(jnp.where(seen, score, masked_score))
+        top = jnp.max(parts[0], axis=1, keepdims=True)
+        for part in parts[1:]:
+            top = jnp.maximum(top, jnp.max(part, axis=1, keepdims=True))
+        parts = [jnp.exp(part - top) for part in parts]
+        total = sum(jnp.sum(part, axis=1, keepdims=True) for part in parts)
+        result = r_buf[:, :, at].reshape(2 * rows, HEAD_DIM).astype(F32)
+        attended = None
+        for dist in range(3):
+            value = kv_buf[dist, h, 1].reshape(2 * rows, HEAD_DIM)
+            term = jnp.dot((parts[dist] / total).astype(BF16), value, preferred_element_type=F32)
+            attended = term if attended is None else attended + term
+        stream = (result + attended).astype(BF16)
+        line_buf[z, h] = stream.reshape(2, rows, HEAD_DIM)
+        pl.when(has_up)(lambda: line_copy(0, z, h).start())
+        pl.when(has_dn)(lambda: line_copy(1, z, h).start())
+        unsent.append((has_up, line_copy(0, z, h)))
+        unsent.append((has_dn, line_copy(1, z, h)))
+
+    for h in range(heads):
+        kv_own(h)
+    kv_relay(0)
+    for i in (2 * heads, 2 * heads + 1):
+        stay[i].wait()
+        landed[i].wait_recv()
+    for h in range(heads):
+        if h + 1 < heads:
+            kv_relay(h + 1)
+        attend(h)
+
+    for step in range(1, planes):
+        below, above = z - step, z + step
+        for h in range(heads):
+
+            @pl.when(below >= 0)
+            def _():
+                line_copy(0, below, h).wait_recv()
+                pl.when(has_up)(lambda: line_copy(0, below, h).start())
+
+            unsent.append(((below >= 0) & has_up, line_copy(0, below, h)))
+
+            @pl.when(above < planes)
+            def _():
+                line_copy(1, above, h).wait_recv()
+                pl.when(has_dn)(lambda: line_copy(1, above, h).start())
+
+            unsent.append(((above < planes) & has_dn, line_copy(1, above, h)))
+
+    for r in range(most):
+        for h in range(heads):
+            x_buf[y, t, pl.ds(r * rows, rows), pl.ds(h * HEAD_DIM, HEAD_DIM)] = line_buf[
+                chosen[r] // 2, h, chosen[r] % 2
+            ]
+
+    def gather(buf, sends, recvs, consume):
+        middle = buf.shape[2] // 2
+        low, high = pl.ds(0, middle), pl.ds(middle, middle)
+
+        def piece(i, at, device):
+            ref = buf.at[at[0], at[1]] if at[2] is None else buf.at[at[0], at[1], at[2]]
+            return remote(ref, ref, sends.at[i], recvs.at[i], device)
+
+        def send(i, at, device):
+            piece(i, at, device).start()
+            unsent.append((None, piece(i, at, device)))
+
+        def take(i, at):
+            piece(i, at, dev_c).wait_recv()
+
+        send(0, (y, t, low), dev_x)
+        send(1, (y, t, high), dev_y)
+        send(2, (y, t, high), dev_x)
+        send(3, (y, t, low), dev_y)
+        send(4, (y, t, None), dev_c)
+        consume(y, t)
+        take(4, (y, tc, None))
+        consume(y, tc)
+        take(0, (y, tx, low))
+        send(5, (y, tx, low), dev_y)
+        send(7, (y, tx, low), dev_c)
+        take(1, (yo, t, high))
+        send(6, (yo, t, high), dev_x)
+        send(8, (yo, t, high), dev_c)
+        take(2, (y, tx, high))
+        send(9, (y, tx, high), dev_c)
+        take(3, (yo, t, low))
+        send(10, (yo, t, low), dev_c)
+        consume(y, tx)
+        consume(yo, t)
+        take(7, (y, txc, low))
+        take(9, (y, txc, high))
+        consume(y, txc)
+        take(8, (yo, tc, high))
+        take(10, (yo, tc, low))
+        consume(yo, tc)
+        take(5, (yo, tx, low))
+        send(11, (yo, tx, low), dev_c)
+        take(6, (yo, tx, high))
+        send(12, (yo, tx, high), dev_c)
+        consume(yo, tx)
+        take(11, (yo, txc, low))
+        take(12, (yo, txc, high))
+        consume(yo, txc)
+
+    acc_buf[...] = jnp.zeros_like(acc_buf)
+    square_buf[...] = jnp.zeros_like(square_buf)
+    for copy in stay[2 * heads + 2 :]:
+        copy.wait()
+
+    def expert_part(py, pt):
+        start = pl.multiple_of((2 * pt + py) * half, half)
+        x = x_buf[py, pt].astype(F32)
+        square_buf[...] += jnp.sum(x * x, axis=1, keepdims=True)
+        scaled = (x * gain_ref[:, pl.ds(start, half)]).astype(BF16)
+        acc_buf[...] += jnp.dot(scaled, w_buf[pl.ds(start, half), :], preferred_element_type=F32)
+
+    gather(x_buf, feat_s, feat_r, expert_part)
+    units = gate_ref.shape[2]
+    features = gain_ref.shape[1]
+    scale = lax.rsqrt(square_buf[...] * (1.0 / features) + epsilon)
+    gate_val = acc_buf[:, pl.ds(0, units)] * scale
+    up_val = acc_buf[:, pl.ds(units, units)] * scale
+    hid_buf[y, t] = (gate_val / (1.0 + jnp.exp(-gate_val)) * up_val).astype(BF16)
+    gather(hid_buf, hid_s, hid_r, lambda py, pt: None)
+
+    landed[2 * heads + 2].wait_recv()
+    branches = []
+    for h in range(2):
+        hidden = jnp.concatenate([hid_buf[h, i] for i in range(hid_buf.shape[1])], axis=1)
+        weight = down_buf[h + 2 * ((y + h) % 2)]
+        branches.append(jnp.dot(hidden, weight, preferred_element_type=F32).astype(BF16))
+    mixed = x_buf[y, t].astype(F32) + branches[0].astype(F32) + branches[1].astype(F32)
+    mix_buf[...] = mixed.astype(BF16).reshape(mix_buf.shape)
+
+    def ret_copy(way, d):
+        if way == 0:
+            return remote(up_out.at[d], up_in.at[d], ret_s.at[0, d], ret_r.at[0, d], dev_up)
+        return remote(dn_out.at[d], dn_in.at[d], ret_s.at[1, d], ret_r.at[1, d], dev_dn)
+
+    def own(b):
+        return mix_buf[slot[b]]
+
+    def pick(flag, a, b):
+        mask = jnp.full(a.shape, flag.astype(jnp.int32), jnp.int32) > 0
+        return jnp.where(mask, a.astype(F32), b.astype(F32)).astype(BF16)
+
+    for step in range(planes - 1):
+        for way, d in ((0, planes - 1 - step), (1, step)):
+            passes = z < d if way == 0 else z > d
+            first = z == 0 if way == 0 else z == planes - 1
+            out, arrived = (up_out, up_in) if way == 0 else (dn_out, dn_in)
+
+            @pl.when(passes & first)
+            def _():
+                for n in range(2):
+                    out[d, n] = own(2 * d + n)
+
+            @pl.when(passes & jnp.logical_not(first))
+            def _():
+                ret_copy(way, d).wait_recv()
+                for n in range(2):
+                    b = 2 * d + n
+                    out[d, n] = pick(expert[b] == z, own(b), arrived[d, n])
+
+            pl.when(passes)(lambda: ret_copy(way, d).start())
+            unsent.append((passes, ret_copy(way, d)))
+
+    last = remote(
+        fin_buf.at[yo], out_ref.at[:, wide(y)], last_s.at[0], last_r.at[0], dev_y
+    )
+    for d in range(planes):
+
+        @pl.when(z == d)
+        def _():
+            if d > 0:
+                ret_copy(0, d).wait_recv()
+            if d < planes - 1:
+                ret_copy(1, d).wait_recv()
+            for n in range(2):
+                b = 2 * d + n
+                value = own(b)
+                if d > 0:
+                    value = pick(expert[b] < z, up_in[d, n], value)
+                if d < planes - 1:
+                    value = pick(expert[b] > z, dn_in[d, n], value)
+                fin_buf[n] = value
+
+    last.start()
+    out_ref[:, wide(y)] = fin_buf[y]
+    remote(
+        out_ref.at[:, wide(yo)], out_ref.at[:, wide(yo)], last_s.at[0], last_r.at[0], dev_y
+    ).wait_recv()
+    last.wait_send()
+    for flag, copy in unsent:
+        if flag is None:
+            copy.wait_send()
+        else:
+            pl.when(flag)(lambda: copy.wait_send())
+
+
+def local(
+    queries, keys, values, residual_in, norm_gain, routing, gate_weight, up_weight, down_weight
+):
+    seq_count = lax.axis_size("seq")
+    tp_count = lax.axis_size("tp")
+    rows, width = queries.shape
+    units = gate_weight.shape[2]
+    planes = seq_count // 2
+    fits = (
+        tp_count == 4
+        and seq_count % 2 == 0
+        and 3 <= planes <= 8
+        and rows == BLOCK
+        and WINDOW == 4 * rows
+        and units == 128
+        and width % (2 * HEAD_DIM) == 0
+    )
+    if not fits:
+        return local_general(
+            queries,
+            keys,
+            values,
+            residual_in,
+            norm_gain,
+            routing,
+            gate_weight,
+            up_weight,
+            down_weight,
+        )
+    half = width // 2
+    heads = half // HEAD_DIM
+    most = min(2 * seq_count // planes, seq_count - planes + 1)
+    features = norm_gain.shape[0]
+    vmem = pl.BlockSpec(memory_space=pltpu.VMEM)
+    anywhere = pl.BlockSpec(memory_space=pl.ANY)
+    dma = pltpu.SemaphoreType.DMA
+    return pl.pallas_call(
+        lambda *refs: layer_kernel(planes, most, *refs),
+        name="layer",
+        out_shape=jax.ShapeDtypeStruct((rows, width), BF16),
+        in_specs=[pl.BlockSpec(memory_space=pltpu.SMEM)]
+        + [anywhere] * 4
+        + [vmem]
+        + [anywhere] * 3,
+        out_specs=vmem,
+        scratch_shapes=[
+            pltpu.VMEM((2, rows, half), BF16),
+            pltpu.VMEM((2, rows, half), BF16),
+            pltpu.VMEM((3, heads, 2, 2, rows, HEAD_DIM), BF16),
+            pltpu.VMEM((planes, heads, 2, rows, HEAD_DIM), BF16),
+            pltpu.VMEM((2, tp_count, most * rows, half), BF16),
+            pltpu.VMEM((features, 2 * units), BF16),
+            pltpu.VMEM((most * rows, 2 * units), F32),
+            pltpu.VMEM((most * rows, 1), F32),
+            pltpu.VMEM((2, tp_count, most * rows, units), BF16),
+            pltpu.VMEM((4, down_weight.shape[1], half), BF16),
+            pltpu.VMEM((most, rows, half), BF16),
+            pltpu.VMEM((planes, 2, rows, half), BF16),
+            pltpu.VMEM((planes, 2, rows, half), BF16),
+            pltpu.VMEM((planes, 2, rows, half), BF16),
+            pltpu.VMEM((planes, 2, rows, half), BF16),
+            pltpu.VMEM((2, rows, half), BF16),
+            dma((2 * heads + 3,)),
+            dma((2 * heads + 3,)),
+            dma((2 * heads + 5,)),
+            dma((2, heads)),
+            dma((2, heads)),
+            dma((2, planes, heads)),
+            dma((2, planes, heads)),
+            dma((13,)),
+            dma((13,)),
+            dma((13,)),
+            dma((13,)),
+            dma((2, planes)),
+            dma((2, planes)),
+            dma((1,)),
+            dma((1,)),
+        ],
+        compiler_params=pltpu.CompilerParams(
+            collective_id=0, has_side_effects=True, vmem_limit_bytes=48 * 1024 * 1024
+        ),
+    )(
+        routing,
+        queries,
+        keys,
+        values,
+        residual_in,
+        norm_gain.reshape(1, features),
+        gate_weight,
+        up_weight,
+        down_weight,
+    )
+
+
 def solution(mesh):
     in_specs = (
         P("seq", "tp"),

time: 242 us -> 116 us (0.48)
  Pallas kernels: 0 us -> 106 us
  blocking collectives: 80.1 us -> 0 us
  starting transfers between devices: 58.8 us -> 0 us
  waiting for transfers between devices: 58.5 us -> 0 us
  between operations: 13.7 us -> 0.02 us
  matrix products: 10.4 us -> 0 us
  other arithmetic: 6.7 us -> 0 us
  local copies, waits for them, and re-layouts: 13.3 us -> 9.63 us
    pallas_call x0 -> x1, Pallas kernels: none -> 106 us  [local(): pl.pallas_call(lambda *refs: layer_kernel(planes, most, *refs), name='lay...]
    all_to_all x3 -> x0, blocking collectives: 72.9 us -> none  [the longest x1 31.5 us: local(): lax.all_to_all(partial_value, 'seq', split_axis=0, concat_axis=0, tiled=T...]
    ppermute x8 -> x0, starting transfers between devices: 42.9 us -> none  [shifted(): return lax.ppermute(block, axis, route)]
    all_gather x1 -> x0, waiting for transfers between devices: 33.6 us -> none  [local(): lax.all_gather(lax.all_to_all(outgoing, 'seq', split_axis=0, concat_axis=...]
    ppermute x8 -> x0, waiting for transfers between devices: 16.4 us -> none  [shifted(): return lax.ppermute(block, axis, route)]
    all_to_all x1 -> x0, starting transfers between devices: 15.9 us -> none  [local(): lax.all_to_all(spread_in, 'seq', split_axis=1, concat_axis=0, tiled=True)]
    all_to_all x1 -> x0, waiting for transfers between devices: 8.5 us -> none  [local(): lax.all_to_all(spread_in, 'seq', split_axis=1, concat_axis=0, tiled=True)]
    all_gather x1 -> x0, blocking collectives: 7.21 us -> none  [local(): hidden_half = lax.all_gather(hidden, 'tp', axis=1, tiled=True)]
  transfers between devices with their start and end apart: 10 -> 0, of which waited for: 4 -> 0; matrix products, arithmetic and copies ran while one was open for 3% -> 0% of each run, Pallas kernels for 0% -> 0%
where the time goes in v1:
time: 116 us
  Pallas kernels  106 us (91%)
  local copies, waits for them, and re-layouts  9.63 us (8%)
    pallas_call x1, Pallas kernels, local(): pl.pallas_call(lambda *refs: layer_kernel(planes, most, *refs), name='lay...  106 us
    unnamed x20, local copies, waits for them, and re-layouts  9.63 us

profile of v1, /device:TPU:0, one launch (start us, length us, event | category | flops | bytes accessed | tf_op | source)
XLA Modules:
  0.0 116.0 jit_solution(2164046637444945979)
XLA Ops:
  0.0 0.0 copy-start.8
  0.0 0.7 copy-done.8
  0.7 0.1 copy.10.refs_0_
  0.7 0.0 copy-start
  0.7 1.2 %copy-done = bf16[1,4096,128]{2,1,0:T(8,128)(2,1)S(1)} copy-done((bf16[1,4096,128]{2,1,0:T(8,128)(2,1)S(1)}, bf16[1,4096,128]{2,1,0:T(8,128)(2,1)}, u32[]{:S(2)}) %copy-start) | copy-done | bytes 1048600
  2.0 0.0 copy-start.1
  2.0 1.2 %copy-done.1 = bf16[1,4096,128]{2,1,0:T(8,128)(2,1)S(1)} copy-done((bf16[1,4096,128]{2,1,0:T(8,128)(2,1)S(1)}, bf16[1,4096,128]{2,1,0:T(8,128)(2,1)}, u32[]{:S(2)}) %copy-start.1) | copy-done | bytes 1048600
  3.2 0.0 copy-start.2
  3.2 1.2 %copy-done.2 = bf16[1,512,1024]{2,1,0:T(8,128)(2,1)S(1)} copy-done((bf16[1,512,1024]{2,1,0:T(8,128)(2,1)S(1)}, bf16[1,512,1024]{2,1,0:T(8,128)(2,1)}, u32[]{:S(2)}) %copy-start.2) | copy-done | bytes 1048600
  4.4 0.0 copy-start.3
  4.4 0.9 copy-done.3
  5.4 0.0 copy-start.4
  5.4 0.9 copy-done.4
  6.3 0.0 copy-start.5
  6.3 0.9 copy-done.5
  7.3 0.0 copy-start.6
  7.3 0.9 copy-done.6
  8.2 0.0 copy-start.7
  8.2 0.7 copy-done.7
  8.9 106.3 %layer.1 = bf16[128,1024]{1,0:T(8,128)(2,1)S(1)} custom-call(s32[8,1]{1,0:T(8,128)S(1)} %copy.10.refs_0_, bf16[128,1024]{1,0:T(8,128)(2,1)S(1)} %copy-done.3, bf16[128,1024]{1,0:T(8,128)(2,1)S(1)} %copy-done.4, bf16[128,1024]{1,0:T(8,128)(2,1)S(1)} %copy-done.5, bf16[128,1024]{1,0:T(8,128)(2,1)S(1)} %copy-done.6, f32[1,4096]{1,0:T(1,128)S(1)} %bitcast.1, ...), custom_call_target="tpu_custom_call" | custom-call | tf_op jit(solution)/shard_map/layer/pallas_call | solution.py:556
  115.3 0.7 copy.12
Async XLA Ops:
  0.0 0.7 copy-start.8
  0.7 1.2 %copy-start = (bf16[1,4096,128]{2,1,0:T(8,128)(2,1)S(1)}, bf16[1,4096,128]{2,1,0:T(8,128)(2,1)}, u32[]{:S(2)}) copy-start(bf16[1,4096,128]{2,1,0:T(8,128)(2,1)} %refs_6_.1) | copy-start | bytes 3145732
  2.0 1.2 %copy-start.1 = (bf16[1,4096,128]{2,1,0:T(8,128)(2,1)S(1)}, bf16[1,4096,128]{2,1,0:T(8,128)(2,1)}, u32[]{:S(2)}) copy-start(bf16[1,4096,128]{2,1,0:T(8,128)(2,1)} %refs_7_.1) | copy-start | bytes 3145732
  3.2 1.2 %copy-start.2 = (bf16[1,512,1024]{2,1,0:T(8,128)(2,1)S(1)}, bf16[1,512,1024]{2,1,0:T(8,128)(2,1)}, u32[]{:S(2)}) copy-start(bf16[1,512,1024]{2,1,0:T(8,128)(2,1)} %refs_8_.1) | copy-start | bytes 3145732
  4.4 0.9 copy-start.3
  5.4 0.9 copy-start.4
  6.3 0.9 copy-start.5
  7.3 0.9 copy-start.6
  8.2 0.7 copy-start.7

commit v2 on v0

--- a/solution.py
+++ b/solution.py
@@ -3,6 +3,8 @@
 import jax
 import jax.numpy as jnp
 from jax import lax
+from jax.experimental import pallas as pl
+from jax.experimental.pallas import tpu as pltpu
 from jax.sharding import PartitionSpec as P
 
 HEAD_DIM = 128
@@ -20,7 +22,7 @@
     return lax.ppermute(block, axis, route)
 
 
-def local(
+def local_general(
     queries, keys, values, residual_in, norm_gain, routing, gate_weight, up_weight, down_weight
 ):
     seq_count = lax.axis_size("seq")
@@ -117,6 +119,619 @@
     return restored.reshape(tok_rows, feat_width)
 
 
+BF16 = jnp.bfloat16
+F32 = jnp.float32
+
+
+def remote(src, dst, send_sem, recv_sem, device):
+    return pltpu.make_async_remote_copy(
+        src_ref=src,
+        dst_ref=dst,
+        send_sem=send_sem,
+        recv_sem=recv_sem,
+        device_id=device,
+        device_id_type=pl.DeviceIdType.MESH,
+    )
+
+
+def layer_kernel(planes, most, arguments, out_ref, scratch):
+    (
+        routing_ref, q_ref, k_ref, v_ref, r_ref, gain_ref, gate_ref, up_ref, down_ref
+    ) = arguments
+    (
+        q_buf,
+        r_buf,
+        kv_buf,
+        line,
+        end_out,
+        end_in,
+        x_buf,
+        w_buf,
+        acc_buf,
+        square_buf,
+        hid_buf,
+        down_buf,
+        mix,
+        end_up,
+        end_dn,
+        up_out,
+        up_in,
+        dn_out,
+        dn_in,
+        fin_buf,
+        pair_s,
+        pair_r,
+        local_s,
+        kvline_s,
+        kvline_r,
+        line_s,
+        line_r,
+        end_s,
+        end_r,
+        feat_s,
+        feat_r,
+        hid_s,
+        hid_r,
+        ret_s,
+        ret_r,
+        edge_s,
+        edge_r,
+        last_s,
+        last_r,
+    ) = scratch
+    rows = q_ref.shape[0]
+    half = q_ref.shape[1] // 2
+    heads = half // HEAD_DIM
+    blocks = 2 * planes
+    me = lax.axis_index("seq")
+    t = lax.axis_index("tp")
+    z = me // 2
+    y = me % 2
+    yo = 1 - y
+    mate = 2 * z + yo
+    tc = t + 1 - 2 * (t % 2)
+    tx = t + 2 - 4 * (t // 2)
+    txc = tx + 1 - 2 * (tx % 2)
+    dev_y, dev_c, dev_x = (mate, t), (me, tc), (me, tx)
+    dev_up, dev_dn = (me + 2, t), (me - 2, t)
+    has_up, has_dn = z < planes - 1, z > 0
+    unsent = []
+
+    barrier = pltpu.get_barrier_semaphore()
+
+    def greet(device):
+        pl.semaphore_signal(
+            barrier, inc=1, device_id=device, device_id_type=pl.DeviceIdType.MESH
+        )
+
+    for device in (dev_y, dev_c, dev_x):
+        greet(device)
+    pl.when(has_up)(lambda: greet(dev_up))
+    pl.when(has_dn)(lambda: greet(dev_dn))
+
+    def cols(which, h):
+        return pl.ds(pl.multiple_of(which * half + h * HEAD_DIM, HEAD_DIM), HEAD_DIM)
+
+    def wide(which):
+        return pl.ds(pl.multiple_of(which * half, half), half)
+
+    stay = []
+    for h in range(heads):
+        stay.append((k_ref.at[:, cols(y, h)], kv_buf.at[0, h, 0, y]))
+        stay.append((v_ref.at[:, cols(y, h)], kv_buf.at[0, h, 1, y]))
+    stay.append((q_ref.at[:, wide(y)], q_buf.at[y]))
+    stay.append((r_ref.at[:, wide(y)], r_buf.at[y]))
+    stay.append((gate_ref.at[0], w_buf.at[:, pl.ds(0, gate_ref.shape[2])]))
+    stay.append((up_ref.at[0], w_buf.at[:, pl.ds(gate_ref.shape[2], gate_ref.shape[2])]))
+    stay.append((down_ref.at[0, :, wide(y)], down_buf.at[y]))
+    stay = [pltpu.make_async_copy(a, b, local_s.at[i]) for i, (a, b) in enumerate(stay)]
+    for copy in stay:
+        copy.start()
+
+    expert = [routing_ref[b, 0] for b in range(blocks)]
+    slot = []
+    for b in range(blocks):
+        count = jnp.int32(0)
+        for j in range(b):
+            count = count + jnp.where(expert[j] == expert[b], 1, 0)
+        slot.append(jnp.minimum(count, most - 1))
+
+    def listing(which):
+        found = []
+        for r in range(most):
+            index = jnp.int32(0)
+            for b in range(blocks):
+                index = jnp.where((expert[b] == which) & (slot[b] == r), b, index)
+            found.append(index)
+        return found
+
+    chosen = listing(z)
+    at_edge = (z == 0) | (z == planes - 1)
+    by_edge = (z == 1) | (z == planes - 2)
+    chosen_edge = listing(jnp.where(z == 1, 0, planes - 1))
+    dev_edge = (jnp.where(z == 1, me - 2, me + 2), t)
+    line_up, line_dn = z < planes - 2, z > 1
+
+    for dist in (1, 2):
+
+        @pl.when(z < dist)
+        def _():
+            kv_buf[dist] = jnp.zeros(kv_buf.shape[1:], kv_buf.dtype)
+
+    pl.semaphore_wait(
+        barrier, 3 + jnp.where(has_up, 1, 0) + jnp.where(has_dn, 1, 0)
+    )
+
+    def pair_copy(i, src, dst):
+        return remote(src, dst, pair_s.at[i], pair_r.at[i], dev_y)
+
+    swap, landed = [], []
+    for h in range(heads):
+        for n, ref in enumerate((k_ref, v_ref)):
+            i = len(swap)
+            swap.append(pair_copy(i, ref.at[:, cols(yo, h)], kv_buf.at[0, h, n, y]))
+            landed.append(pair_copy(i, kv_buf.at[0, h, n, yo], kv_buf.at[0, h, n, yo]))
+    for ref, buf in ((q_ref, q_buf), (r_ref, r_buf)):
+        i = len(swap)
+        swap.append(pair_copy(i, ref.at[:, wide(yo)], buf.at[y]))
+        landed.append(pair_copy(i, buf.at[yo], buf.at[yo]))
+    i = len(swap)
+    swap.append(pair_copy(i, down_ref.at[0, :, wide(yo)], down_buf.at[y + 2]))
+    landed.append(pair_copy(i, down_buf.at[yo + 2], down_buf.at[yo + 2]))
+    for copy in swap:
+        copy.start()
+        unsent.append((None, copy))
+
+    def kv_copy(dist, h):
+        return remote(
+            kv_buf.at[dist, h],
+            kv_buf.at[dist + 1, h],
+            kvline_s.at[dist, h],
+            kvline_r.at[dist, h],
+            dev_up,
+        )
+
+    def kv_own(h):
+        for i in (2 * h, 2 * h + 1):
+            stay[i].wait()
+            landed[i].wait_recv()
+        pl.when(has_up)(lambda: kv_copy(0, h).start())
+        unsent.append((has_up, kv_copy(0, h)))
+
+    def kv_relay(h):
+        pl.when(has_dn)(lambda: kv_copy(0, h).wait_recv())
+        pl.when(has_dn & has_up)(lambda: kv_copy(1, h).start())
+        unsent.append((has_dn & has_up, kv_copy(1, h)))
+
+    def line_copy(way, plane, h):
+        return remote(
+            line[h].at[plane],
+            line[h].at[plane],
+            line_s.at[way, plane, h],
+            line_r.at[way, plane, h],
+            dev_up if way == 0 else dev_dn,
+        )
+
+    query_at = lax.broadcasted_iota(jnp.int32, (2 * rows, 2 * rows), 0)
+    key_at = lax.broadcasted_iota(jnp.int32, (2 * rows, 2 * rows), 1)
+
+    def attend(h):
+        pl.when(z > 1)(lambda: kv_copy(1, h).wait_recv())
+        at = pl.ds(h * HEAD_DIM, HEAD_DIM)
+        query = q_buf[:, :, at].reshape(2 * rows, HEAD_DIM)
+        parts = []
+        for dist in range(3):
+            key = kv_buf[dist, h, 0].reshape(2 * rows, HEAD_DIM)
+            score = lax.dot_general(
+                query, key, (((1,), (1,)), ((), ())), preferred_element_type=F32
+            ) * (1.0 / math.sqrt(HEAD_DIM))
+            gap = query_at - key_at + 2 * rows * dist
+            seen = (gap >= 0) & (gap < WINDOW) & (jnp.full(gap.shape, z, jnp.int32) >= dist)
+            parts.append(jnp.where(seen, score, masked_score))
+        top = jnp.max(parts[0], axis=1, keepdims=True)
+        for part in parts[1:]:
+            top = jnp.maximum(top, jnp.max(part, axis=1, keepdims=True))
+        parts = [jnp.exp(part - top) for part in parts]
+        total = sum(jnp.sum(part, axis=1, keepdims=True) for part in parts)
+        result = r_buf[:, :, at].reshape(2 * rows, HEAD_DIM).astype(F32)
+        attended = None
+        for dist in range(3):
+            value = kv_buf[dist, h, 1].reshape(2 * rows, HEAD_DIM)
+            term = jnp.dot((parts[dist] / total).astype(BF16), value, preferred_element_type=F32)
+            attended = term if attended is None else attended + term
+        stream = (result + attended).astype(BF16)
+        line[h][z] = stream.reshape(2, rows, HEAD_DIM)
+        pl.when(line_up)(lambda: line_copy(0, z, h).start())
+        pl.when(line_dn)(lambda: line_copy(1, z, h).start())
+        unsent.append((line_up, line_copy(0, z, h)))
+        unsent.append((line_dn, line_copy(1, z, h)))
+
+    def end_copy(h):
+        return remote(end_out[h], end_in[h], end_s.at[h], end_r.at[h], dev_edge)
+
+    def pick(flag, a, b):
+        mask = jnp.full(a.shape, flag.astype(jnp.int32), jnp.int32) > 0
+        return jnp.where(mask, a.astype(F32), b.astype(F32)).astype(BF16)
+
+    def spread(h):
+        for step in range(1, planes):
+            below, above = z - step, z + step
+            from_below = (below >= 0) & (z < planes - 1)
+            from_above = (above < planes) & (z > 0)
+
+            @pl.when(from_below)
+            def _():
+                line_copy(0, below, h).wait_recv()
+                pl.when(line_up)(lambda: line_copy(0, below, h).start())
+
+            @pl.when(from_above)
+            def _():
+                line_copy(1, above, h).wait_recv()
+                pl.when(line_dn)(lambda: line_copy(1, above, h).start())
+
+            unsent.append((from_below & line_up, line_copy(0, below, h)))
+            unsent.append((from_above & line_dn, line_copy(1, above, h)))
+
+        @pl.when(by_edge)
+        def _():
+            for r in range(most):
+                end_out[h][r] = line[h][chosen_edge[r] // 2, chosen_edge[r] % 2]
+            end_copy(h).start()
+
+        unsent.append((by_edge, end_copy(h)))
+
+        @pl.when(at_edge)
+        def _():
+            end_copy(h).wait_recv()
+            for r in range(most):
+                x_buf[y, t, h, pl.ds(r * rows, rows)] = pick(
+                    chosen[r] // 2 == z, line[h][z, chosen[r] % 2], end_in[h][r]
+                )
+
+        @pl.when(jnp.logical_not(at_edge))
+        def _():
+            for r in range(most):
+                x_buf[y, t, h, pl.ds(r * rows, rows)] = line[h][chosen[r] // 2, chosen[r] % 2]
+
+    def gatherer(buf, sends, recvs, h):
+        middle = buf.shape[3] // 2
+        low, high, whole = pl.ds(0, middle), pl.ds(middle, middle), pl.ds(0, 2 * middle)
+
+        def piece(i, at, device):
+            ref = buf.at[at[0], at[1], h, at[2]]
+            return remote(ref, ref, sends.at[i, h], recvs.at[i, h], device)
+
+        def send(i, at, device):
+            piece(i, at, device).start()
+            unsent.append((None, piece(i, at, device)))
+
+        def take(i, at):
+            piece(i, at, dev_c).wait_recv()
+
+        def first():
+            send(0, (y, t, low), dev_x)
+            send(1, (y, t, high), dev_y)
+            send(2, (y, t, high), dev_x)
+            send(3, (y, t, low), dev_y)
+            send(4, (y, t, whole), dev_c)
+
+        def second():
+            take(0, (y, tx, low))
+            send(5, (y, tx, low), dev_y)
+            send(7, (y, tx, low), dev_c)
+            take(1, (yo, t, high))
+            send(6, (yo, t, high), dev_x)
+            send(8, (yo, t, high), dev_c)
+            take(2, (y, tx, high))
+            send(9, (y, tx, high), dev_c)
+            take(3, (yo, t, low))
+            send(10, (yo, t, low), dev_c)
+
+        def third():
+            take(5, (yo, tx, low))
+            send(11, (yo, tx, low), dev_c)
+            take(6, (yo, tx, high))
+            send(12, (yo, tx, high), dev_c)
+
+        def near():
+            take(4, (y, tc, whole))
+            take(7, (y, txc, low))
+            take(9, (y, txc, high))
+            take(8, (yo, tc, high))
+            take(10, (yo, tc, low))
+
+        def far():
+            take(11, (yo, txc, low))
+            take(12, (yo, txc, high))
+
+        return first, second, third, near, far
+
+    def expert_parts(parts, pair):
+        left, right = [], []
+        square = square_buf[...]
+        for py, pt in parts:
+            for h in (2 * pair, 2 * pair + 1):
+                start = pl.multiple_of((2 * pt + py) * half + h * HEAD_DIM, HEAD_DIM)
+                x = x_buf[py, pt, h].astype(F32)
+                square = square + jnp.sum(x * x, axis=1, keepdims=True)
+                left.append((x * gain_ref[:, pl.ds(start, HEAD_DIM)]).astype(BF16))
+                right.append(w_buf[pl.ds(start, HEAD_DIM), :])
+        square_buf[...] = square
+        acc_buf[...] += jnp.dot(
+            jnp.concatenate(left, axis=1),
+            jnp.concatenate(right, axis=0),
+            preferred_element_type=F32,
+        )
+
+    stages = [gatherer(x_buf, feat_s, feat_r, h) for h in range(heads)]
+    most_parts = [(y, t), (y, tc), (y, tx), (yo, t), (y, txc), (yo, tc)]
+    rest_parts = [(yo, tx), (yo, txc)]
+    for h in range(heads):
+        kv_own(h)
+    kv_relay(0)
+    for i in (2 * heads, 2 * heads + 1):
+        stay[i].wait()
+        landed[i].wait_recv()
+    for turn in range(heads + 3):
+        if turn + 1 < heads:
+            kv_relay(turn + 1)
+        if turn < heads:
+            attend(turn)
+        if turn == heads:
+            acc_buf[...] = jnp.zeros_like(acc_buf)
+            square_buf[...] = jnp.zeros_like(square_buf)
+            for copy in stay[2 * heads + 2 :]:
+                copy.wait()
+        if 0 <= turn - 1 < heads:
+            spread(turn - 1)
+            stages[turn - 1][0]()
+        if 0 <= turn - 2 < heads:
+            stages[turn - 2][1]()
+        if 0 <= turn - 3 < heads:
+            h = turn - 3
+            if h == heads - 1:
+                stages[h][3]()
+                expert_parts(most_parts, h // 2)
+            stages[h][2]()
+            if h < heads - 1:
+                stages[h][3]()
+            stages[h][4]()
+            if h == heads - 1:
+                expert_parts(rest_parts, h // 2)
+            elif h % 2 == 1:
+                expert_parts(most_parts + rest_parts, h // 2)
+    units = gate_ref.shape[2]
+    features = gain_ref.shape[1]
+    scale = lax.rsqrt(square_buf[...] * (1.0 / features) + epsilon)
+    gate_val = acc_buf[:, pl.ds(0, units)] * scale
+    up_val = acc_buf[:, pl.ds(units, units)] * scale
+    hid_buf[y, t, 0] = (gate_val / (1.0 + jnp.exp(-gate_val)) * up_val).astype(BF16)
+    for stage in gatherer(hid_buf, hid_s, hid_r, 0):
+        stage()
+
+    chunks = len(mix)
+    span = half // chunks
+    per = span // HEAD_DIM
+
+    def edge_copy(way, c):
+        dst = end_up[c] if way == 0 else end_dn[c]
+        return remote(
+            mix[c], dst, edge_s.at[way, c], edge_r.at[way, c], dev_up if way == 0 else dev_dn
+        )
+
+    def ret_copy(way, d, c):
+        out, arrived = (up_out, up_in) if way == 0 else (dn_out, dn_in)
+        return remote(
+            out.at[c, d],
+            arrived.at[c, d],
+            ret_s.at[way, d, c],
+            ret_r.at[way, d, c],
+            dev_up if way == 0 else dev_dn,
+        )
+
+    landed[2 * heads + 2].wait_recv()
+    hidden = [
+        jnp.concatenate([hid_buf[h, i, 0] for i in range(hid_buf.shape[1])], axis=1)
+        for h in range(2)
+    ]
+    for c in range(chunks):
+        total = jnp.concatenate(
+            [x_buf[y, t, c * per + i] for i in range(per)], axis=1
+        ).astype(F32)
+        for h in range(2):
+            weight = down_buf[h + 2 * ((y + h) % 2), :, pl.ds(c * span, span)]
+            branch = jnp.dot(hidden[h], weight, preferred_element_type=F32).astype(BF16)
+            total = total + branch.astype(F32)
+        mix[c][...] = total.astype(BF16).reshape(most, rows, span)
+        pl.when(z == 0)(lambda: edge_copy(0, c).start())
+        pl.when(z == planes - 1)(lambda: edge_copy(1, c).start())
+        unsent.append((z == 0, edge_copy(0, c)))
+        unsent.append((z == planes - 1, edge_copy(1, c)))
+
+    for c in range(chunks):
+        pl.when(z == 1)(lambda: edge_copy(0, c).wait_recv())
+        pl.when(z == planes - 2)(lambda: edge_copy(1, c).wait_recv())
+        for step in range(planes - 1):
+            for way, d in ((0, planes - 1 - step), (1, step)):
+                passes = (z < d) & (z > 0) if way == 0 else (z > d) & (z < planes - 1)
+                near = z == 1 if way == 0 else z == planes - 2
+                end = end_up[c] if way == 0 else end_dn[c]
+                out, arrived = (up_out, up_in) if way == 0 else (dn_out, dn_in)
+
+                @pl.when(passes & near)
+                def _():
+                    for n in range(2):
+                        b = 2 * d + n
+                        out[c, d, n] = pick(expert[b] == z, mix[c][slot[b]], end[slot[b]])
+
+                @pl.when(passes & jnp.logical_not(near))
+                def _():
+                    ret_copy(way, d, c).wait_recv()
+                    for n in range(2):
+                        b = 2 * d + n
+                        out[c, d, n] = pick(expert[b] == z, mix[c][slot[b]], arrived[c, d, n])
+
+                pl.when(passes)(lambda: ret_copy(way, d, c).start())
+                unsent.append((passes, ret_copy(way, d, c)))
+
+    def finish(which, c):
+        return pl.ds(pl.multiple_of(which * half + c * span, span), span)
+
+    def last_copy(c):
+        return remote(
+            fin_buf.at[c, yo], out_ref.at[:, finish(y, c)], last_s.at[c], last_r.at[c], dev_y
+        )
+
+    for c in range(chunks):
+        for d in range(planes):
+
+            @pl.when(z == d)
+            def _():
+                if d > 1:
+                    ret_copy(0, d, c).wait_recv()
+                if d < planes - 2:
+                    ret_copy(1, d, c).wait_recv()
+                for n in range(2):
+                    b = 2 * d + n
+                    value = mix[c][slot[b]]
+                    if d > 0:
+                        value = pick(
+                            expert[b] < z, up_in[c, d, n] if d > 1 else end_up[c][slot[b]], value
+                        )
+                    if d < planes - 1:
+                        value = pick(
+                            expert[b] > z,
+                            dn_in[c, d, n] if d < planes - 2 else end_dn[c][slot[b]],
+                            value,
+                        )
+                    fin_buf[c, n] = value
+
+        last_copy(c).start()
+        unsent.append((None, last_copy(c)))
+        out_ref[:, finish(y, c)] = fin_buf[c, y]
+    for c in range(chunks):
+        mine = out_ref.at[:, finish(yo, c)]
+        remote(mine, mine, last_s.at[c], last_r.at[c], dev_y).wait_recv()
+    for flag, copy in unsent:
+        if flag is None:
+            copy.wait_send()
+        else:
+            pl.when(flag)(lambda: copy.wait_send())
+
+
+def local(
+    queries, keys, values, residual_in, norm_gain, routing, gate_weight, up_weight, down_weight
+):
+    seq_count = lax.axis_size("seq")
+    tp_count = lax.axis_size("tp")
+    rows, width = queries.shape
+    units = gate_weight.shape[2]
+    planes = seq_count // 2
+    fits = (
+        tp_count == 4
+        and seq_count % 2 == 0
+        and 4 <= planes <= 8
+        and rows == BLOCK
+        and WINDOW == 4 * rows
+        and units == 128
+        and width % (8 * HEAD_DIM) == 0
+    )
+    if not fits:
+        return local_general(
+            queries,
+            keys,
+            values,
+            residual_in,
+            norm_gain,
+            routing,
+            gate_weight,
+            up_weight,
+            down_weight,
+        )
+    half = width // 2
+    heads = half // HEAD_DIM
+    most = min(2 * seq_count // planes, seq_count - planes + 1)
+    chunks = 2
+    span = half // chunks
+    vmem = pl.BlockSpec(memory_space=pltpu.VMEM)
+    anywhere = pl.BlockSpec(memory_space=pl.ANY)
+    dma = pltpu.SemaphoreType.DMA
+
+    def room(*shape, kind=BF16):
+        return pltpu.VMEM(shape, kind)
+
+    scratch = (
+        room(2, rows, half),
+        room(2, rows, half),
+        room(3, heads, 2, 2, rows, HEAD_DIM),
+        [room(planes, 2, rows, HEAD_DIM) for _ in range(heads)],
+        [room(most, rows, HEAD_DIM) for _ in range(heads)],
+        [room(most, rows, HEAD_DIM) for _ in range(heads)],
+        room(2, tp_count, heads, most * rows, HEAD_DIM),
+        room(norm_gain.shape[0], 2 * units),
+        room(most * rows, 2 * units, kind=F32),
+        room(most * rows, 1, kind=F32),
+        room(2, tp_count, 1, most * rows, units),
+        room(4, down_weight.shape[1], half),
+        [room(most, rows, span) for _ in range(chunks)],
+        [room(most, rows, span) for _ in range(chunks)],
+        [room(most, rows, span) for _ in range(chunks)],
+        room(chunks, planes, 2, rows, span),
+        room(chunks, planes, 2, rows, span),
+        room(chunks, planes, 2, rows, span),
+        room(chunks, planes, 2, rows, span),
+        room(chunks, 2, rows, span),
+        dma((2 * heads + 3,)),
+        dma((2 * heads + 3,)),
+        dma((2 * heads + 5,)),
+        dma((2, heads)),
+        dma((2, heads)),
+        dma((2, planes, heads)),
+        dma((2, planes, heads)),
+        dma((heads,)),
+        dma((heads,)),
+        dma((13, heads)),
+        dma((13, heads)),
+        dma((13, 1)),
+        dma((13, 1)),
+        dma((2, planes, chunks)),
+        dma((2, planes, chunks)),
+        dma((2, chunks)),
+        dma((2, chunks)),
+        dma((chunks,)),
+        dma((chunks,)),
+    )
+    flat, tree = jax.tree.flatten(scratch, is_leaf=lambda leaf: not isinstance(leaf, (list, tuple)))
+
+    def kernel(*refs):
+        layer_kernel(planes, most, refs[:9], refs[9], jax.tree.unflatten(tree, refs[10:]))
+
+    return pl.pallas_call(
+        kernel,
+        name="layer",
+        out_shape=jax.ShapeDtypeStruct((rows, width), BF16),
+        in_specs=[pl.BlockSpec(memory_space=pltpu.SMEM)]
+        + [anywhere] * 4
+        + [vmem]
+        + [anywhere] * 3,
+        out_specs=vmem,
+        scratch_shapes=flat,
+        compiler_params=pltpu.CompilerParams(
+            collective_id=0, has_side_effects=True, vmem_limit_bytes=48 * 1024 * 1024
+        ),
+    )(
+        routing,
+        queries,
+        keys,
+        values,
+        residual_in,
+        norm_gain.reshape(1, -1),
+        gate_weight,
+        up_weight,
+        down_weight,
+    )
+
+
 def solution(mesh):
     in_specs = (
         P("seq", "tp"),

time: 242 us -> 124 us (0.51)
  Pallas kernels: 0 us -> 114 us
  blocking collectives: 80.1 us -> 0 us
  starting transfers between devices: 58.8 us -> 0 us
  waiting for transfers between devices: 58.5 us -> 0 us
  between operations: 13.7 us -> 0.02 us
  matrix products: 10.4 us -> 0 us
  other arithmetic: 6.7 us -> 0 us
  local copies, waits for them, and re-layouts: 13.3 us -> 9.63 us
    pallas_call x0 -> x1, Pallas kernels: none -> 114 us  [local(): pl.pallas_call(kernel, name='layer', out_shape=jax.ShapeDtypeStruct((rows...]
    all_to_all x3 -> x0, blocking collectives: 72.9 us -> none  [the longest x1 31.5 us: local(): lax.all_to_all(partial_value, 'seq', split_axis=0, concat_axis=0, tiled=T...]
    ppermute x8 -> x0, starting transfers between devices: 42.9 us -> none  [shifted(): return lax.ppermute(block, axis, route)]
    all_gather x1 -> x0, waiting for transfers between devices: 33.6 us -> none  [local(): lax.all_gather(lax.all_to_all(outgoing, 'seq', split_axis=0, concat_axis=...]
    ppermute x8 -> x0, waiting for transfers between devices: 16.4 us -> none  [shifted(): return lax.ppermute(block, axis, route)]
    all_to_all x1 -> x0, starting transfers between devices: 15.9 us -> none  [local(): lax.all_to_all(spread_in, 'seq', split_axis=1, concat_axis=0, tiled=True)]
    all_to_all x1 -> x0, waiting for transfers between devices: 8.5 us -> none  [local(): lax.all_to_all(spread_in, 'seq', split_axis=1, concat_axis=0, tiled=True)]
    all_gather x1 -> x0, blocking collectives: 7.21 us -> none  [local(): hidden_half = lax.all_gather(hidden, 'tp', axis=1, tiled=True)]
  transfers between devices with their start and end apart: 10 -> 0, of which waited for: 4 -> 0; matrix products, arithmetic and copies ran while one was open for 3% -> 0% of each run, Pallas kernels for 0% -> 0%
where the time goes in v2:
time: 124 us; the launch traced here: 123 us
  Pallas kernels  114 us (92%)
  local copies, waits for them, and re-layouts  9.63 us (8%)
    pallas_call x1, Pallas kernels, local(): pl.pallas_call(kernel, name='layer', out_shape=jax.ShapeDtypeStruct((rows...  114 us
    unnamed x20, local copies, waits for them, and re-layouts  9.63 us

profile of v2, /device:TPU:0, one launch (start us, length us, event | category | flops | bytes accessed | tf_op | source)
XLA Modules:
  0.0 123.5 jit_solution(13700847898271064314)
XLA Ops:
  0.0 0.0 copy-start.8
  0.0 0.7 copy-done.8
  0.7 0.1 copy.10.refs_0_
  0.7 0.0 copy-start
  0.7 1.2 copy-done
  2.0 0.0 copy-start.1
  2.0 1.2 copy-done.1
  3.2 0.0 copy-start.2
  3.2 1.2 copy-done.2
  4.4 0.0 copy-start.3
  4.4 0.9 copy-done.3
  5.4 0.0 copy-start.4
  5.4 0.9 copy-done.4
  6.3 0.0 copy-start.5
  6.3 0.9 copy-done.5
  7.3 0.0 copy-start.6
  7.3 0.9 copy-done.6
  8.2 0.0 copy-start.7
  8.2 0.7 copy-done.7
  8.9 113.8 %layer.1 = bf16[128,1024]{1,0:T(8,128)(2,1)S(1)} custom-call(s32[8,1]{1,0:T(8,128)S(1)} %copy.10.refs_0_, bf16[128,1024]{1,0:T(8,128)(2,1)S(1)} %copy-done.3, bf16[128,1024]{1,0:T(8,128)(2,1)S(1)} %copy-done.4, bf16[128,1024]{1,0:T(8,128)(2,1)S(1)} %copy-done.5, bf16[128,1024]{1,0:T(8,128)(2,1)S(1)} %copy-done.6, f32[1,4096]{1,0:T(1,128)S(1)} %bitcast.1, ...), custom_call_target="tpu_custom_call" | custom-call | tf_op jit(solution)/shard_map/layer/pallas_call | solution.py:709
  122.8 0.7 copy.12
Async XLA Ops:
  0.0 0.7 copy-start.8
  0.7 1.2 copy-start
  2.0 1.2 copy-start.1
  3.2 1.2 copy-start.2
  4.4 0.9 copy-start.3
  5.4 0.9 copy-start.4
  6.3 0.9 copy-start.5
  7.3 0.9 copy-start.6
  8.2 0.7 copy-start.7

commit v3 on v2

--- a/solution.py
+++ b/solution.py
@@ -312,35 +312,50 @@
             dev_up if way == 0 else dev_dn,
         )
 
-    query_at = lax.broadcasted_iota(jnp.int32, (2 * rows, 2 * rows), 0)
-    key_at = lax.broadcasted_iota(jnp.int32, (2 * rows, 2 * rows), 1)
+    row_at = lax.broadcasted_iota(jnp.int32, (rows, rows), 0)
+    col_at = lax.broadcasted_iota(jnp.int32, (rows, rows), 1)
+    behind = [jnp.where(z >= dist, 0.0, masked_score).astype(F32) for dist in range(3)]
 
     def attend(h):
         pl.when(z > 1)(lambda: kv_copy(1, h).wait_recv())
         at = pl.ds(h * HEAD_DIM, HEAD_DIM)
-        query = q_buf[:, :, at].reshape(2 * rows, HEAD_DIM)
-        parts = []
-        for dist in range(3):
-            key = kv_buf[dist, h, 0].reshape(2 * rows, HEAD_DIM)
-            score = lax.dot_general(
-                query, key, (((1,), (1,)), ((), ())), preferred_element_type=F32
-            ) * (1.0 / math.sqrt(HEAD_DIM))
-            gap = query_at - key_at + 2 * rows * dist
-            seen = (gap >= 0) & (gap < WINDOW) & (jnp.full(gap.shape, z, jnp.int32) >= dist)
-            parts.append(jnp.where(seen, score, masked_score))
-        top = jnp.max(parts[0], axis=1, keepdims=True)
-        for part in parts[1:]:
-            top = jnp.maximum(top, jnp.max(part, axis=1, keepdims=True))
-        parts = [jnp.exp(part - top) for part in parts]
-        total = sum(jnp.sum(part, axis=1, keepdims=True) for part in parts)
-        result = r_buf[:, :, at].reshape(2 * rows, HEAD_DIM).astype(F32)
-        attended = None
-        for dist in range(3):
-            value = kv_buf[dist, h, 1].reshape(2 * rows, HEAD_DIM)
-            term = jnp.dot((parts[dist] / total).astype(BF16), value, preferred_element_type=F32)
-            attended = term if attended is None else attended + term
-        stream = (result + attended).astype(BF16)
-        line[h][z] = stream.reshape(2, rows, HEAD_DIM)
+        count = WINDOW // rows
+        for n in range(2):
+            query = q_buf[n, :, at]
+            places = []
+            for back in range(count + 1):
+                dist = (back - n + 1) // 2
+                places.append((dist, (n - back) % 2))
+            parts = []
+            for back, (dist, block) in enumerate(places):
+                part = lax.dot_general(
+                    query,
+                    kv_buf[dist, h, 0, block],
+                    (((1,), (1,)), ((), ())),
+                    preferred_element_type=F32,
+                )
+                if back == 0:
+                    part = jnp.where(col_at <= row_at, part, masked_score)
+                if back == count:
+                    part = jnp.where(col_at > row_at, part, masked_score)
+                if dist > 0:
+                    part = part + behind[dist]
+                parts.append(part)
+            top = parts[0]
+            for part in parts[1:]:
+                top = jnp.maximum(top, part)
+            top = jnp.max(top, axis=1, keepdims=True)
+            parts = [jnp.exp((part - top) * (1.0 / math.sqrt(HEAD_DIM))) for part in parts]
+            total = parts[0]
+            for part in parts[1:]:
+                total = total + part
+            share = 1.0 / jnp.sum(total, axis=1, keepdims=True)
+            attended = jnp.dot(
+                jnp.concatenate([(part * share).astype(BF16) for part in parts], axis=1),
+                jnp.concatenate([kv_buf[dist, h, 1, block] for dist, block in places], axis=0),
+                preferred_element_type=F32,
+            )
+            line[h][z, n] = (r_buf[n, :, at].astype(F32) + attended).astype(BF16)
         pl.when(line_up)(lambda: line_copy(0, z, h).start())
         pl.when(line_dn)(lambda: line_copy(1, z, h).start())
         unsent.append((line_up, line_copy(0, z, h)))
@@ -548,31 +563,29 @@
         unsent.append((z == 0, edge_copy(0, c)))
         unsent.append((z == planes - 1, edge_copy(1, c)))
 
-    for c in range(chunks):
-        pl.when(z == 1)(lambda: edge_copy(0, c).wait_recv())
-        pl.when(z == planes - 2)(lambda: edge_copy(1, c).wait_recv())
+    def relay(c, close):
+        if close:
+            pl.when(z == 1)(lambda: edge_copy(0, c).wait_recv())
+            pl.when(z == planes - 2)(lambda: edge_copy(1, c).wait_recv())
         for step in range(planes - 1):
             for way, d in ((0, planes - 1 - step), (1, step)):
                 passes = (z < d) & (z > 0) if way == 0 else (z > d) & (z < planes - 1)
                 near = z == 1 if way == 0 else z == planes - 2
                 end = end_up[c] if way == 0 else end_dn[c]
                 out, arrived = (up_out, up_in) if way == 0 else (dn_out, dn_in)
-
-                @pl.when(passes & near)
+                here = passes & near if close else passes & jnp.logical_not(near)
+
+                @pl.when(here)
                 def _():
+                    if not close:
+                        ret_copy(way, d, c).wait_recv()
                     for n in range(2):
                         b = 2 * d + n
-                        out[c, d, n] = pick(expert[b] == z, mix[c][slot[b]], end[slot[b]])
-
-                @pl.when(passes & jnp.logical_not(near))
-                def _():
-                    ret_copy(way, d, c).wait_recv()
-                    for n in range(2):
-                        b = 2 * d + n
-                        out[c, d, n] = pick(expert[b] == z, mix[c][slot[b]], arrived[c, d, n])
-
-                pl.when(passes)(lambda: ret_copy(way, d, c).start())
-                unsent.append((passes, ret_copy(way, d, c)))
+                        other = end[slot[b]] if close else arrived[c, d, n]
+                        out[c, d, n] = pick(expert[b] == z, mix[c][slot[b]], other)
+                    ret_copy(way, d, c).start()
+
+                unsent.append((here, ret_copy(way, d, c)))
 
     def finish(which, c):
         return pl.ds(pl.multiple_of(which * half + c * span, span), span)
@@ -582,7 +595,7 @@
             fin_buf.at[c, yo], out_ref.at[:, finish(y, c)], last_s.at[c], last_r.at[c], dev_y
         )
 
-    for c in range(chunks):
+    def arrive(c):
         for d in range(planes):
 
             @pl.when(z == d)
@@ -609,6 +622,14 @@
         last_copy(c).start()
         unsent.append((None, last_copy(c)))
         out_ref[:, finish(y, c)] = fin_buf[c, y]
+    relay(0, True)
+    for c in range(chunks):
+        if c + 1 < chunks:
+            relay(c + 1, True)
+        relay(c, False)
+        if c > 0:
+            arrive(c - 1)
+    arrive(chunks - 1)
     for c in range(chunks):
         mine = out_ref.at[:, finish(yo, c)]
         remote(mine, mine, last_s.at[c], last_r.at[c], dev_y).wait_recv()
@@ -651,10 +672,10 @@
     half = width // 2
     heads = half // HEAD_DIM
     most = min(2 * seq_count // planes, seq_count - planes + 1)
-    chunks = 2
+    chunks = 4
     span = half // chunks
     vmem = pl.BlockSpec(memory_space=pltpu.VMEM)
-    anywhere = pl.BlockSpec(memory_space=pl.ANY)
+    anywhere = pl.BlockSpec(memory_space=pltpu.MemorySpace.HBM)
     dma = pltpu.SemaphoreType.DMA
 
     def room(*shape, kind=BF16):

time: 124 us -> 110 us (0.89)
  Pallas kernels: 114 us -> 100 us
    pallas_call x1, Pallas kernels: 114 us -> 100 us  [local(): pl.pallas_call(kernel, name='layer', out_shape=jax.ShapeDtypeStruct((rows...]
where the time goes in v3:
time: 110 us
  Pallas kernels  100 us (91%)
  local copies, waits for them, and re-layouts  9.63 us (9%)
    pallas_call x1, Pallas kernels, local(): pl.pallas_call(kernel, name='layer', out_shape=jax.ShapeDtypeStruct((rows...  100 us
    unnamed x20, local copies, waits for them, and re-layouts  9.63 us

profile of v3, /device:TPU:0, one launch (start us, length us, event | category | flops | bytes accessed | tf_op | source)
XLA Modules:
  0.0 109.9 jit_solution(8733884117378830321)
XLA Ops:
  0.0 0.0 copy-start.8
  0.0 0.7 copy-done.8
  0.7 0.1 copy.10.refs_0_
  0.7 0.0 copy-start
  0.7 1.2 %copy-done = bf16[1,4096,128]{2,1,0:T(8,128)(2,1)S(1)} copy-done((bf16[1,4096,128]{2,1,0:T(8,128)(2,1)S(1)}, bf16[1,4096,128]{2,1,0:T(8,128)(2,1)}, u32[]{:S(2)}) %copy-start) | copy-done | bytes 1048600
  2.0 0.0 copy-start.1
  2.0 1.2 %copy-done.1 = bf16[1,4096,128]{2,1,0:T(8,128)(2,1)S(1)} copy-done((bf16[1,4096,128]{2,1,0:T(8,128)(2,1)S(1)}, bf16[1,4096,128]{2,1,0:T(8,128)(2,1)}, u32[]{:S(2)}) %copy-start.1) | copy-done | bytes 1048600
  3.2 0.0 copy-start.2
  3.2 1.2 %copy-done.2 = bf16[1,512,1024]{2,1,0:T(8,128)(2,1)S(1)} copy-done((bf16[1,512,1024]{2,1,0:T(8,128)(2,1)S(1)}, bf16[1,512,1024]{2,1,0:T(8,128)(2,1)}, u32[]{:S(2)}) %copy-start.2) | copy-done | bytes 1048600
  4.4 0.0 copy-start.3
  4.4 0.9 copy-done.3
  5.4 0.0 copy-start.4
  5.4 0.9 copy-done.4
  6.3 0.0 copy-start.5
  6.3 0.9 copy-done.5
  7.3 0.0 copy-start.6
  7.3 0.9 copy-done.6
  8.2 0.0 copy-start.7
  8.2 0.7 copy-done.7
  8.9 100.2 %layer.1 = bf16[128,1024]{1,0:T(8,128)(2,1)S(1)} custom-call(s32[8,1]{1,0:T(8,128)S(1)} %copy.10.refs_0_, bf16[128,1024]{1,0:T(8,128)(2,1)S(1)} %copy-done.3, bf16[128,1024]{1,0:T(8,128)(2,1)S(1)} %copy-done.4, bf16[128,1024]{1,0:T(8,128)(2,1)S(1)} %copy-done.5, bf16[128,1024]{1,0:T(8,128)(2,1)S(1)} %copy-done.6, f32[1,4096]{1,0:T(1,128)S(1)} %bitcast.1, ...), custom_call_target="tpu_custom_call" | custom-call | tf_op jit(solution)/shard_map/layer/pallas_call | solution.py:730
  109.2 0.7 copy.12
Async XLA Ops:
  0.0 0.7 copy-start.8
  0.7 1.2 %copy-start = (bf16[1,4096,128]{2,1,0:T(8,128)(2,1)S(1)}, bf16[1,4096,128]{2,1,0:T(8,128)(2,1)}, u32[]{:S(2)}) copy-start(bf16[1,4096,128]{2,1,0:T(8,128)(2,1)} %refs_6_.1) | copy-start | bytes 3145732
  2.0 1.2 %copy-start.1 = (bf16[1,4096,128]{2,1,0:T(8,128)(2,1)S(1)}, bf16[1,4096,128]{2,1,0:T(8,128)(2,1)}, u32[]{:S(2)}) copy-start(bf16[1,4096,128]{2,1,0:T(8,128)(2,1)} %refs_7_.1) | copy-start | bytes 3145732
  3.2 1.2 %copy-start.2 = (bf16[1,512,1024]{2,1,0:T(8,128)(2,1)S(1)}, bf16[1,512,1024]{2,1,0:T(8,128)(2,1)}, u32[]{:S(2)}) copy-start(bf16[1,512,1024]{2,1,0:T(8,128)(2,1)} %refs_8_.1) | copy-start | bytes 3145732
  4.4 0.9 copy-start.3
  5.4 0.9 copy-start.4
  6.3 0.9 copy-start.5
  7.3 0.9 copy-start.6
  8.2 0.7 copy-start.7

commit v4 on v3

--- a/solution.py
+++ b/solution.py
@@ -228,7 +228,7 @@
     for copy in stay:
         copy.start()
 
-    expert = [routing_ref[b, 0] for b in range(blocks)]
+    expert = [routing_ref[b] for b in range(blocks)]
     slot = []
     for b in range(blocks):
         count = jnp.int32(0)
@@ -738,10 +738,10 @@
         out_specs=vmem,
         scratch_shapes=flat,
         compiler_params=pltpu.CompilerParams(
-            collective_id=0, has_side_effects=True, vmem_limit_bytes=48 * 1024 * 1024
+            collective_id=0, has_side_effects=True, vmem_limit_bytes=67043328
         ),
     )(
-        routing,
+        routing.reshape(-1),
         queries,
         keys,
         values,

time: 110 us -> 103 us (0.936)
  local copies, waits for them, and re-layouts: 9.63 us -> 1.67 us
    unnamed x20 -> x1, local copies, waits for them, and re-layouts: 9.63 us -> 1.67 us
where the time goes in v4:
time: 103 us
  Pallas kernels  101 us (98%)
  local copies, waits for them, and re-layouts  1.67 us (2%)
    pallas_call x1, Pallas kernels, local(): pl.pallas_call(kernel, name='layer', out_shape=jax.ShapeDtypeStruct((rows...  101 us

profile of v4, /device:TPU:0, one launch (start us, length us, event | category | flops | bytes accessed | tf_op | source)
XLA Modules:
  0.0 102.9 jit_solution(9180506516127105578)
XLA Ops:
  0.0 101.3 %layer.1 = bf16[128,1024]{1,0:T(8,128)(2,1)} custom-call(s32[8]{0:T(128)} %bitcast.3, bf16[128,1024]{1,0:T(8,128)(2,1)} %refs_1_.1, bf16[128,1024]{1,0:T(8,128)(2,1)} %refs_2_.1, bf16[128,1024]{1,0:T(8,128)(2,1)} %refs_3_.1, bf16[128,1024]{1,0:T(8,128)(2,1)} %refs_4_.1, f32[1,4096]{1,0:T(1,128)} %bitcast.2, bf16[1,4096,128]{2,1,0:T(8,128)(2,1)} %refs_6_.1, ...), custom_call_target="tpu_custom_call" | custom-call | tf_op jit(solution)/shard_map/layer/pallas_call | solution.py:730
  101.3 1.7 %copy.11 = bf16[128,1024]{1,0:T(8,128)(2,1)} copy(bf16[128,1024]{1,0:T(8,128)(2,1)} %layer.1) | data formatting | bytes 524288
